TPU v7x, 32 devices: a whole 2x2x4 slice. The times are simulated.
32 devices in a mesh: rows: 8 (over z, y), mp: 4 (over x, core).
Axes of the slice: x: 2, y: 2, z: 4, core: 2. Of those that a mesh axis runs over, the one named last changes fastest.
Arguments:
- calib: bfloat16 [512, 8192], P('rows', 'mp'), may hold values from -40 to 40
- weight: bfloat16 [8192, 8192], P('rows', 'mp'), may hold values from -6 to 6
- inverse_factor: float32 [8192, 8192], P('rows', 'mp'), may hold values from -10 to 12, as said below
- pruned_blocks: int32 [7], replicated, may hold values from 0 to 63, as said below
Outputs:
- pruned_weight: bfloat16 [8192, 8192], P('rows', 'mp')
- next_gram: float32 [8192, 8192], P('rows', 'mp')
Inputs may be any that keep to these rules, and one draw needn't show every extreme that they name: `pruned_blocks`: 7 distinct block numbers in any order; block b holds rows b * 128 to b * 128 + 127. `inverse_factor`: symmetric and positive definite.
All inputs are finite; a program needn't handle non-finite values.
Results may differ from a plain program's by a relative error of at most 0.0095.
Values may be sent and summed in bfloat16 or wider, within the bound.
A program may use at most 128 MiB of HBM per device.

v0:
```python
import functools

import jax
import jax.numpy as jnp
from jax import lax
from jax.experimental import pallas as pl
from jax.experimental.pallas import tpu as pltpu
from jax.sharding import PartitionSpec as P

BLOCK = 128
SUB = 8
GROUP = 4


def split3(value):
    first = value.astype(jnp.bfloat16)
    rest = value - first.astype(jnp.float32)
    second = rest.astype(jnp.bfloat16)
    third = (rest - second.astype(jnp.float32)).astype(jnp.bfloat16)
    return first, second, third


def sweep_block(tiles):
    lane = lax.broadcasted_iota(jnp.int32, (SUB, BLOCK), 1)
    sublane = lax.broadcasted_iota(jnp.int32, (SUB, BLOCK), 0)
    wide = (SUB, BLOCK)
    for p in range(0, BLOCK, GROUP):
        own, s = p // SUB, p % SUB
        rows = [
            jnp.broadcast_to(tiles[own][s + a : s + a + 1, :], wide) for a in range(GROUP)
        ]
        small = {}
        for a in range(GROUP):
            for b in range(a, GROUP):
                small[a, b] = jnp.broadcast_to(rows[a][:, p + b : p + b + 1], wide)
        for k in range(GROUP):
            inv = 1.0 / small[k, k]
            old = {a: small[min(a, k), max(a, k)] for a in range(GROUP) if a != k}
            scaled = {a: value * inv for a, value in old.items()}
            for a in old:
                for b in old:
                    if a <= b:
                        small[a, b] = small[a, b] - old[a] * scaled[b]
                small[min(a, k), max(a, k)] = scaled[a]
            small[k, k] = -inv
        pivots = [lane == p + a for a in range(GROUP)]
        updates = []
        for a in range(GROUP):
            update = -small[0, a] * rows[0]
            for b in range(1, GROUP):
                update = update - small[min(a, b), max(a, b)] * rows[b]
            for b in range(GROUP):
                update = jnp.where(pivots[b], small[min(a, b), max(a, b)], update)
            updates.append(update)
        inside = (lane >= p) & (lane < p + GROUP)
        new = []
        for t in range(len(tiles)):
            value = jnp.where(inside, 0.0, tiles[t])
            for a in range(GROUP):
                column = jnp.broadcast_to(tiles[t][:, p + a : p + a + 1], wide)
                value = value - column * updates[a]
            if t == own:
                for a in range(GROUP):
                    value = jnp.where(sublane == s + a, updates[a], value)
            new.append(value)
        tiles = new
    return tiles


def invert_kernel(low_ref, out_ref, neg_ref, rhs_ref, pivot_ref):
    count = out_ref.shape[0] // BLOCK
    at = 0
    for i in range(count):
        for j in range(i + 1):
            block = low_ref[:, at : at + BLOCK]
            at += BLOCK
            out_ref[i * BLOCK : (i + 1) * BLOCK, j * BLOCK : (j + 1) * BLOCK] = block
            if j < i:
                out_ref[j * BLOCK : (j + 1) * BLOCK, i * BLOCK : (i + 1) * BLOCK] = block.T

    def stage(k, carry):
        here = pl.ds(pl.multiple_of(k * BLOCK, BLOCK), BLOCK)
        diag = out_ref[here, here]
        tiles = [diag[t * SUB : (t + 1) * SUB, :] for t in range(BLOCK // SUB)]
        tiles = sweep_block(tiles)
        for t in range(BLOCK // SUB):
            neg_ref[t * SUB : (t + 1) * SUB, :] = tiles[t]
        neg = neg_ref[...]
        r1, r2, r3 = split3(out_ref[here, :])
        a1, a2, a3 = split3(-neg)
        pivot_ref[...] = jnp.dot(
            jnp.concatenate([a1, a1, a2, a2, a1, a3], axis=1),
            jnp.concatenate([r1, r2, r1, r2, r3, r1], axis=0),
            preferred_element_type=jnp.float32,
        )
        pivot_ref[:, here] = neg
        b1, b2, b3 = split3(pivot_ref[...])
        for slot, part in enumerate((b1, b2, b1, b2, b3, b1)):
            rhs_ref[slot * BLOCK : (slot + 1) * BLOCK, :] = part

        def update(i, inner):
            rows = pl.ds(pl.multiple_of(i * BLOCK, BLOCK), BLOCK)
            c1, c2, c3 = split3(out_ref[rows, here])
            out_ref[rows, here] = jnp.zeros((BLOCK, BLOCK), jnp.float32)
            out_ref[rows, :] -= jnp.dot(
                jnp.concatenate([c1, c1, c2, c2, c1, c3], axis=1),
                rhs_ref[...],
                preferred_element_type=jnp.float32,
            )
            return inner

        lax.fori_loop(0, count, update, 0)
        out_ref[here, :] = pivot_ref[...]
        return carry

    lax.fori_loop(0, count, stage, 0)


def minus_inverse(low, order):
    vmem = pl.BlockSpec(memory_space=pltpu.VMEM)
    return pl.pallas_call(
        invert_kernel,
        out_shape=jax.ShapeDtypeStruct((order, order), jnp.float32),
        in_specs=[vmem],
        out_specs=vmem,
        scratch_shapes=[
            pltpu.VMEM((BLOCK, BLOCK), jnp.float32),
            pltpu.VMEM((6 * BLOCK, order), jnp.bfloat16),
            pltpu.VMEM((BLOCK, order), jnp.float32),
        ],
        compiler_params=pltpu.CompilerParams(vmem_limit_bytes=32 * 1024 * 1024),
        cost_estimate=pl.CostEstimate(
            flops=60_000_000_000, bytes_accessed=2 * order * order * 4, transcendentals=0
        ),
    )(low)


def pick_columns_kernel(places_ref, factor_ref, columns_ref, low_ref):
    j = pl.program_id(0)
    columns_ref[...] = jnp.where(places_ref[1, j] != 0, factor_ref[...], 0.0)
    for i in range(places_ref.shape[1]):

        @pl.when(i >= j)
        def _():
            rows = pl.ds(pl.multiple_of(places_ref[2, i] * BLOCK, BLOCK), BLOCK)
            lanes = pl.ds(pl.multiple_of((i * (i + 1) // 2 + j) * BLOCK, BLOCK), BLOCK)
            low_ref[:, lanes] = jnp.where(places_ref[3, i] != 0, columns_ref[rows, :], 0.0)


def pick_columns(places, factor):
    count = places.shape[1]
    rows = factor.shape[0]
    lanes = count * (count + 1) // 2 * BLOCK
    return pl.pallas_call(
        pick_columns_kernel,
        out_shape=(
            jax.ShapeDtypeStruct((rows, count * BLOCK), jnp.float32),
            jax.ShapeDtypeStruct((BLOCK, lanes), jnp.float32),
        ),
        grid_spec=pltpu.PrefetchScalarGridSpec(
            num_scalar_prefetch=1,
            grid=(count,),
            in_specs=[pl.BlockSpec((rows, BLOCK), lambda j, places: (0, places[0, j]))],
            out_specs=(
                pl.BlockSpec((rows, BLOCK), lambda j, places: (0, j)),
                pl.BlockSpec((BLOCK, lanes), lambda j, places: (0, 0)),
            ),
        ),
    )(places, factor)


def pick_rows_kernel(places_ref, weight_ref, out_ref):
    inside = places_ref[3, pl.program_id(0)] != 0
    value = weight_ref[...].astype(jnp.float32)
    out_ref[...] = jnp.where(inside, value, 0.0).astype(jnp.bfloat16)


def pick_rows(places, weight):
    count = places.shape[1]
    width = weight.shape[1]
    return pl.pallas_call(
        pick_rows_kernel,
        out_shape=jax.ShapeDtypeStruct((count * BLOCK, width), jnp.bfloat16),
        grid_spec=pltpu.PrefetchScalarGridSpec(
            num_scalar_prefetch=1,
            grid=(count,),
            in_specs=[pl.BlockSpec((BLOCK, width), lambda i, places: (places[2, i], 0))],
            out_specs=pl.BlockSpec((BLOCK, width), lambda i, places: (i, 0)),
        ),
    )(places, weight)


def gram_kernel(token_count, left_ref, right_ref, out_ref):
    out_ref[...] = lax.dot_general(
        left_ref[...],
        right_ref[0],
        (((0,), (0,)), ((), ())),
        preferred_element_type=jnp.float32,
    ) / token_count


def gram_of(left, right, token_count):
    tokens, rows = left.shape
    parts, _, width = right.shape
    tile = min(rows, 256)
    return pl.pallas_call(
        functools.partial(gram_kernel, token_count),
        grid=(parts, rows // tile),
        in_specs=[
            pl.BlockSpec((tokens, tile), lambda c, i: (0, i)),
            pl.BlockSpec((1, tokens, width), lambda c, i: (c, 0, 0)),
        ],
        out_specs=pl.BlockSpec((tile, width), lambda c, i: (i, c)),
        out_shape=jax.ShapeDtypeStruct((rows, parts * width), jnp.float32),
    )(left, right)


def shards(calib, weight, inverse_factor, pruned_blocks):
    rows_dev = weight.shape[0]
    width_dev = weight.shape[1]
    row_parts = lax.axis_size("rows")
    mp_parts = lax.axis_size("mp")
    full_width = width_dev * mp_parts
    row_start = lax.axis_index("rows") * rows_dev
    col_start = lax.axis_index("mp") * width_dev
    starts = pruned_blocks * BLOCK
    block_count = pruned_blocks.shape[0]
    col_offsets = starts - col_start
    row_offsets = starts - row_start
    places = jnp.stack(
        [
            jnp.clip(col_offsets, 0, width_dev - BLOCK) // BLOCK,
            ((col_offsets >= 0) & (col_offsets < width_dev)).astype(jnp.int32),
            jnp.clip(row_offsets, 0, rows_dev - BLOCK) // BLOCK,
            ((row_offsets >= 0) & (row_offsets < rows_dev)).astype(jnp.int32),
        ]
    ).astype(jnp.int32)
    columns, own_low = pick_columns(places, inverse_factor)
    low = lax.psum(own_low, ("rows", "mp"))
    own_columns = lax.psum_scatter(columns, "mp", scatter_dimension=0, tiled=True)
    all_calib = lax.all_gather(calib, "rows", axis=0, tiled=True)
    low, own_kept = lax.optimization_barrier((low, pick_rows(places, weight)))
    kept_rows = lax.psum(own_kept, "rows")

    negative = minus_inverse(low, block_count * BLOCK)
    negative, all_calib, own_columns = lax.optimization_barrier((negative, all_calib, own_columns))
    own_factors = -lax.dot_general(
        own_columns,
        negative,
        (((1,), (0,)), ((), ())),
        precision=lax.Precision.HIGHEST,
        preferred_element_type=jnp.float32,
    )
    factors = lax.all_gather(own_factors.astype(jnp.bfloat16), "mp", axis=0, tiled=True)
    update = lax.dot_general(
        factors, kept_rows, (((1,), (0,)), ((), ())), preferred_element_type=jnp.float32
    )
    block_ids = (row_start + jnp.arange(rows_dev, dtype=jnp.int32)) // BLOCK
    pruned = jnp.any(block_ids[:, None] == pruned_blocks[None, :], axis=1)
    pruned_weight = jnp.where(
        pruned[:, None], 0.0, weight.astype(jnp.float32) - update
    ).astype(jnp.bfloat16)
    out_scale = float(full_width) ** (-0.5)
    partial_value = lax.dot_general(
        all_calib, pruned_weight, (((1,), (1,)), ((), ())), preferred_element_type=jnp.float32
    )
    token_count = partial_value.shape[0]
    own_rows = lax.psum_scatter(
        (partial_value * out_scale).astype(jnp.bfloat16), "mp", scatter_dimension=0, tiled=True
    )
    per_col = row_parts // mp_parts
    pairs = []
    for r in range(row_parts):
        for m in range(mp_parts):
            target = ((r % per_col) * mp_parts + m) * mp_parts + r // per_col
            pairs.append((r * mp_parts + m, target))
    moved = lax.ppermute(own_rows, ("rows", "mp"), pairs)
    left = lax.all_gather(own_rows, "mp", axis=0, tiled=True)
    right = lax.all_gather(moved, "rows", axis=0, tiled=False)
    right = right.reshape(per_col, token_count, rows_dev)
    gram_block = gram_of(left, right, token_count)
    return (pruned_weight, gram_block)


def solution(mesh):
    return jax.shard_map(
        shards,
        mesh=mesh,
        in_specs=(P("rows", "mp"), P("rows", "mp"), P("rows", "mp"), P()),
        out_specs=(P("rows", "mp"), P("rows", "mp")),
        check_vma=False,
    )
```

profile of v0, /device:TPU:0, one launch (start us, length us, event | category | flops | bytes accessed | tf_op | source)
XLA Modules:
  0.0 436.7 jit_solution(15148825526252918606)
XLA Ops:
  8.0 0.7 fusion.4
  8.7 0.7 fusion.7
  9.4 0.6 pad_add_fusion.places_ref
  10.0 7.7 %shard_map.59 = (f32[1024,896]{1,0:T(8,128)}, f32[128,3584]{1,0:T(8,128)}) custom-call(s32[4,7]{1,0:T(4,128)} %pad_add_fusion.places_ref, f32[1024,2048]{1,0:T(8,128)} %factor_ref.1), custom_call_target="tpu_custom_call" | custom-call | tf_op jit(solution)/shard_map/pallas_call | solution.py:154
  17.7 0.0 all-gather.6.cloned.1.call-start
  17.8 0.5 all-gather.6.cloned.1.call-update
  18.4 0.7 reduce-scatter.3.cloned.1.call-update
  19.1 6.6 %shard_map.60 = bf16[896,2048]{1,0:T(8,128)(2,1)} custom-call(s32[4,7]{1,0:T(4,128)} %pad_add_fusion.places_ref, bf16[1024,2048]{1,0:T(8,128)(2,1)} %weight_ref.1), custom_call_target="tpu_custom_call" | custom-call | tf_op jit(solution)/shard_map/pallas_call | solution.py:181
  25.8 138.9 %all-reduce.3.cloned.1.call-done.low_ref = f32[128,3584]{1,0:T(8,128)} async-done(((f32[128,3584]{1,0:T(8,128)}), f32[128,3584]{1,0:T(8,128)}) %all-reduce.3.cloned.1.call-update) | async-done | bytes 1835024 | tf_op jit(solution)/shard_map/psum | solution.py:239
  164.8 1.5 copy-done
  166.3 62.7 %shard_map.61 = f32[896,896]{1,0:T(8,128)S(1)} custom-call(f32[128,3584]{1,0:T(8,128)S(1)} %copy-done), custom_call_target="tpu_custom_call" | custom-call | flops 60000002048 | bytes 6422528 | tf_op jit(solution)/shard_map/pallas_call | solution.py:121
  229.1 5.5 %fusion = bf16[256,896]{1,0:T(8,128)(2,1)} fusion(f32[256,896]{1,0:T(8,128)} %reduce-scatter.3.cloned.1.call-done, f32[896,896]{1,0:T(8,128)S(1)} %shard_map.61), kind=kOutput, calls=%fused_computation.3 | convolution fusion | flops 2466709504 | bytes 4587520 | tf_op jit(solution)/shard_map/dot_general | solution.py:247
  234.7 0.2 reduce-scatter.5.cloned.1.call-start
  234.9 0.1 compare_reduce_fusion
  235.0 71.2 %all-reduce.5.cloned.1.call-done = bf16[896,2048]{1,0:T(8,128)(2,1)} async-done(((bf16[896,2048]{1,0:T(8,128)(2,1)}), bf16[896,2048]{1,0:T(8,128)(2,1)}) %all-reduce.5.cloned.1.call-update) | async-done | bytes 3670032 | tf_op jit(solution)/shard_map/psum | solution.py:243
  306.2 8.4 %select_convert_fusion = bf16[1024,2048]{1,0:T(8,128)(2,1)S(1)} fusion(bf16[1024,2048]{1,0:T(8,128)(2,1)} %weight_ref.1, pred[1024]{0:T(1024)(128)(4,1)S(1)} %compare_reduce_fusion, bf16[1024,896]{1,0:T(8,128)(2,1)} %all-gather.8.cloned.1.call-done, bf16[896,2048]{1,0:T(8,128)(2,1)} %all-reduce.5.cloned.1.call-done), kind=kOutput, calls=%fused_computation | convolution fusion | flops 3766484992 | bytes 13894656 | tf_op jit(solution)/shard_map/dot_general | solution.py:255
  314.6 2.0 copy-done.4
  316.6 3.4 multiply_convert_fusion
  320.0 23.9 %reduce-scatter.5.cloned.1.call-done = bf16[128,1024]{1,0:T(8,128)(2,1)} async-done(((bf16[512,1024]{1,0:T(8,128)(2,1)}), bf16[128,1024]{1,0:T(8,128)(2,1)}) %reduce-scatter.5.cloned.1.call-update) | async-done | bytes 262160 | tf_op jit(solution)/shard_map/reduce_scatter | solution.py:268
  344.0 1.6 collective-permute-start
  345.6 0.7 copy-done.1
  346.4 20.1 %all-gather.10.cloned.1.call-done.left_ref = bf16[512,1024]{1,0:T(8,128)(2,1)} async-done(((bf16[128,1024]{1,0:T(8,128)(2,1)}), bf16[512,1024]{1,0:T(8,128)(2,1)}) %all-gather.10.cloned.1.call-update) | async-done | bytes 1048592 | tf_op jit(solution)/shard_map/all_gather | solution.py:278
  366.4 53.9 %all-gather.12.cloned.1.call-done = bf16[1024,1024]{1,0:T(8,128)(2,1)} async-done(((bf16[128,1024]{1,0:T(8,128)(2,1)}), bf16[1024,1024]{1,0:T(8,128)(2,1)}) %all-gather.12.cloned.1.call-update) | async-done | bytes 2097168 | tf_op jit(solution)/shard_map/all_gather | solution.py:279
  420.3 8.9 %shard_map.62 = f32[1024,2048]{1,0:T(8,128)} custom-call(bf16[512,1024]{1,0:T(8,128)(2,1)} %all-gather.10.cloned.1.call-done.left_ref, bf16[2,512,1024]{2,1,0:T(8,128)(2,1)} %bitcast.15), custom_call_target="tpu_custom_call" | custom-call | tf_op jit(solution)/shard_map/pallas_call | solution.py:206
  (24 shorter events, 0.4 us)
Async XLA Ops:
  8.0 156.7 %all-reduce.3.cloned.1.call-start = ((), (), s32[]{:S(2)}) async-start(), calls=%async_computation.2 | async-start | bytes 3670016 | tf_op jit(solution)/shard_map/psum | solution.py:239
  17.7 211.3 %all-gather.6.cloned.1.call-start = ((), (), s32[]{:S(2)}) async-start(), calls=%async_computation.3 | async-start | bytes 2359296 | tf_op jit(solution)/shard_map/all_gather | solution.py:241
  18.3 210.8 %reduce-scatter.3.cloned.1.call-start = ((), (), s32[]{:S(2)}) async-start(), calls=%async_computation.4 | async-start | bytes 4587520 | tf_op jit(solution)/shard_map/reduce_scatter | solution.py:240
  19.1 287.1 %all-reduce.5.cloned.1.call-start = ((), (), s32[]{:S(2)}) async-start(), calls=%async_computation.6 | async-start | bytes 7340032 | tf_op jit(solution)/shard_map/psum | solution.py:243
  164.7 141.5 %all-gather.8.cloned.1.call-start = ((), (), s32[]{:S(2)}) async-start(), calls=%async_computation.5 | async-start | bytes 2293760 | tf_op jit(solution)/shard_map/all_gather | solution.py:254
  164.8 1.5 copy-start
  229.0 5.9 %copy-start.2 = (s32[7]{0:T(128)S(1)}, s32[7]{0:T(128)}, u32[]{:S(2)}) copy-start(s32[7]{0:T(128)} %param.7) | copy-start | bytes 88
  234.7 109.3 %reduce-scatter.5.cloned.1.call-start = ((), (), s32[]{:S(2)}) async-start(), calls=%async_computation.7 | async-start | bytes 1310720 | tf_op jit(solution)/shard_map/reduce_scatter | solution.py:268
  235.0 81.6 %copy-start.3 = (bf16[512,2048]{1,0:T(8,128)(2,1)S(1)}, bf16[512,2048]{1,0:T(8,128)(2,1)}, u32[]{:S(2)}) copy-start(bf16[512,2048]{1,0:T(8,128)(2,1)} %all-gather.6.cloned.1.call-done) | copy-start | bytes 6291460
  314.6 2.0 copy-start.4
  320.0 46.5 %all-gather.10.cloned.1.call-start = ((), (), s32[]{:S(2)}) async-start(), calls=%async_computation.8 | async-start | bytes 1310720 | tf_op jit(solution)/shard_map/all_gather | solution.py:278
  344.0 76.3 %all-gather.12.cloned.1.call-start = ((), (), s32[]{:S(2)}) async-start(), calls=%async_computation.9 | async-start | bytes 2359296 | tf_op jit(solution)/shard_map/all_gather | solution.py:279
  344.0 1.6 collective-permute-start
  345.6 0.7 copy-start.1
Sparse Core Ops, SparseCore 0:
  17.9 146.7 all-reduce.2
  167.8 40.1 reduce-scatter.2
  234.8 20.0 all-gather.7
  320.1 23.8 reduce-scatter.4
  345.4 21.0 all-gather.9
  369.0 51.2 all-gather.11
Sparse Core Ops, SparseCore 1:
  20.4 53.4 all-gather.5
  164.8 141.3 all-reduce.4
where the time goes:
time: 437 us
  waiting for transfers between devices  309 us (71%)
  Pallas kernels  86.1 us (20%)
  matrix products  17.2 us (4%)
  between operations  15.6 us (4%)
    psum x1, waiting for transfers between devices, shards(): low = lax.psum(own_low, ('rows', 'mp'))  139 us
    psum x1, waiting for transfers between devices, shards(): kept_rows = lax.psum(own_kept, 'rows')  71.2 us
    pallas_call x1, Pallas kernels, minus_inverse(): pl.pallas_call(invert_kernel, out_shape=jax.ShapeDtypeStruct((order, orde...  62.7 us
    all_gather x1, waiting for transfers between devices, shards(): right = lax.all_gather(moved, 'rows', axis=0, tiled=False)  53.9 us
    reduce_scatter x1, waiting for transfers between devices, shards(): lax.psum_scatter((partial_value * out_scale).astype(jnp.bfloat16), 'mp',...  23.9 us
    all_gather x1, waiting for transfers between devices, shards(): left = lax.all_gather(own_rows, 'mp', axis=0, tiled=True)  20.1 us
    pallas_call x1, Pallas kernels, gram_of(): pl.pallas_call(functools.partial(gram_kernel, token_count), grid=(parts,...  8.93 us
  transfers between devices with their start and end apart: 9, of which 5 were waited for; matrix products, arithmetic and copies ran while one was open for 1% of the time, Pallas kernels for 16%

commit v1 on v0

v1 whole, which is shorter than its diff:
```python
import functools

import jax
import jax.numpy as jnp
from jax import lax
from jax.experimental import pallas as pl
from jax.experimental.pallas import tpu as pltpu
from jax.sharding import PartitionSpec as P

BLOCK = 128
SUB = 8
GROUP = 4
MIB = 1024 * 1024
VMEM = pl.BlockSpec(memory_space=pltpu.VMEM)
SMEM = pl.BlockSpec(memory_space=pltpu.SMEM)


def split3(value):
    first = value.astype(jnp.bfloat16)
    rest = value - first.astype(jnp.float32)
    second = rest.astype(jnp.bfloat16)
    third = (rest - second.astype(jnp.float32)).astype(jnp.bfloat16)
    return first, second, third


def sweep_block(tiles):
    lane = lax.broadcasted_iota(jnp.int32, (SUB, BLOCK), 1)
    sublane = lax.broadcasted_iota(jnp.int32, (SUB, BLOCK), 0)
    wide = (SUB, BLOCK)
    for p in range(0, BLOCK, GROUP):
        own, s = p // SUB, p % SUB
        rows = [
            jnp.broadcast_to(tiles[own][s + a : s + a + 1, :], wide) for a in range(GROUP)
        ]
        small = {}
        for a in range(GROUP):
            for b in range(a, GROUP):
                small[a, b] = jnp.broadcast_to(rows[a][:, p + b : p + b + 1], wide)
        for k in range(GROUP):
            inv = 1.0 / small[k, k]
            old = {a: small[min(a, k), max(a, k)] for a in range(GROUP) if a != k}
            scaled = {a: value * inv for a, value in old.items()}
            for a in old:
                for b in old:
                    if a <= b:
                        small[a, b] = small[a, b] - old[a] * scaled[b]
                small[min(a, k), max(a, k)] = scaled[a]
            small[k, k] = -inv
        pivots = [lane == p + a for a in range(GROUP)]
        updates = []
        for a in range(GROUP):
            update = -small[0, a] * rows[0]
            for b in range(1, GROUP):
                update = update - small[min(a, b), max(a, b)] * rows[b]
            for b in range(GROUP):
                update = jnp.where(pivots[b], small[min(a, b), max(a, b)], update)
            updates.append(update)
        inside = (lane >= p) & (lane < p + GROUP)
        new = []
        for t in range(len(tiles)):
            value = jnp.where(inside, 0.0, tiles[t])
            for a in range(GROUP):
                column = jnp.broadcast_to(tiles[t][:, p + a : p + a + 1], wide)
                value = value - column * updates[a]
            if t == own:
                for a in range(GROUP):
                    value = jnp.where(sublane == s + a, updates[a], value)
            new.append(value)
        tiles = new
    return tiles


def bits_of(count):
    return count.bit_length() - 1


def flip(index, k):
    return index + (1 - 2 * ((index // 2**k) % 2)) * 2**k


def reversed_bits(index, count):
    value = 0
    for k in range(bits_of(count)):
        value = value * 2 + (index // 2**k) % 2
    return value


def ordered_bits(index, order):
    value = 0
    for k in order:
        value = value * 2 + (index // 2**k) % 2
    return value


def span(start, size, unit):
    return pl.ds(pl.multiple_of(start, unit), size)


class Links:
    def __init__(self, send_sem, recv_sem):
        self.send_sem = send_sem
        self.recv_sem = recv_sem
        self.used = 0

    def copy(self, src, dst, device):
        at = self.used
        self.used += 1
        return lambda: pltpu.make_async_remote_copy(
            src_ref=src,
            dst_ref=dst,
            send_sem=self.send_sem.at[at],
            recv_sem=self.recv_sem.at[at],
            device_id=device,
            device_id_type=pl.DeviceIdType.MESH,
        )


def greet(devices):
    barrier = pltpu.get_barrier_semaphore()
    for device in devices:
        pl.semaphore_signal(
            barrier, inc=1, device_id=device, device_id_type=pl.DeviceIdType.MESH
        )
    pl.semaphore_wait(barrier, len(devices))


def everyone():
    row_parts, mp_parts = lax.axis_size("rows"), lax.axis_size("mp")
    r, m = lax.axis_index("rows"), lax.axis_index("mp")
    devices = [{"mp": flip(m, k)} for k in range(bits_of(mp_parts))]
    devices += [{"rows": lax.rem(r + d, row_parts)} for d in range(1, row_parts)]
    return devices


def add_rows(out_ref, out_at, left_ref, left_at, right_ref, right_at, size, unit):
    chunk = unit

    def body(t, carry):
        step = pl.multiple_of(t * chunk, chunk)
        a = left_ref[span(left_at + step, chunk, 16), :].astype(jnp.float32)
        b = right_ref[span(right_at + step, chunk, 16), :].astype(jnp.float32)
        out_ref[span(out_at + step, chunk, 16), :] = (a + b).astype(out_ref.dtype)
        return carry

    lax.fori_loop(0, size // chunk, body, 0)


def reduce_sizes(piece, row_parts, mp_parts):
    size = piece * row_parts * mp_parts
    return (size - piece * row_parts) + (row_parts - 1) * piece


def reduce_count(row_parts, mp_parts):
    return 2 * bits_of(mp_parts) + 2 * (row_parts - 1)


def reduce_steps(links, src, acc, recv, out, piece):
    row_parts, mp_parts = lax.axis_size("rows"), lax.axis_size("mp")
    r, m = lax.axis_index("rows"), lax.axis_index("mp")
    stages = []
    size, base, off = piece * row_parts * mp_parts, 0, 0
    held = []
    for k in range(bits_of(mp_parts)):
        held.append((base, size))
        size //= 2
        bit = (m // 2**k) % 2
        keep, send = base + bit * size, base + (1 - bit) * size
        source = src if k == 0 else acc
        copy = links.copy(
            source.at[span(send, size, 16)],
            recv.at[pl.ds(off, size)],
            {"mp": flip(m, k)},
        )

        def merge(source=source, keep=keep, off=off, size=size):
            add_rows(acc, keep, source, keep, recv, off, size, piece)

        stages.append(([copy], merge))
        base, off = keep, off + size
    copies = []
    for d in range(1, row_parts):
        to = lax.rem(r + d, row_parts)
        copies.append(
            links.copy(
                acc.at[span(base + to * piece, piece, 16)],
                recv.at[pl.ds(off + (d - 1) * piece, piece)],
                {"rows": to},
            )
        )

    def total(base=base, off=off):
        mine = span(base + r * piece, piece, 16)
        value = acc[mine, :].astype(jnp.float32)
        for d in range(1, row_parts):
            value = value + recv[pl.ds(off + (d - 1) * piece, piece), :].astype(jnp.float32)
        out[mine, :] = value.astype(out.dtype)

    stages.append((copies, total))
    copies = []
    for d in range(1, row_parts):
        mine = out.at[span(base + r * piece, piece, 16)]
        copies.append(links.copy(mine, mine, {"rows": lax.rem(r + d, row_parts)}))
    stages.append((copies, None))
    for k in reversed(range(bits_of(mp_parts))):
        mine = out.at[span(base, size, 16)]
        stages.append(([links.copy(mine, mine, {"mp": flip(m, k)})], None))
        base, size = held[k]
    return stages


def steps_of(stages):
    steps = []
    for s in range(len(stages) + 1):

        def step(s=s):
            if s > 0:
                for copy in stages[s - 1][0]:
                    copy().wait()
                if stages[s - 1][1] is not None:
                    stages[s - 1][1]()
            if s < len(stages):
                for copy in stages[s][0]:
                    copy().start()

        steps.append(step)
    return steps


def run_steps(*lists):
    for s in range(max(len(one) for one in lists)):
        for one in lists:
            if s < len(one):
                one[s]()


def sum_low_kernel(src_ref, out_ref, acc_ref, recv_ref, send_sem, recv_sem):
    greet(everyone())
    links = Links(send_sem, recv_sem)
    pieces = lax.axis_size("rows") * lax.axis_size("mp")
    piece = src_ref.shape[0] // pieces
    run_steps(steps_of(reduce_steps(links, src_ref, acc_ref, recv_ref, out_ref, piece)))


def sum_low(low):
    row_parts, mp_parts = lax.axis_size("rows"), lax.axis_size("mp")
    piece = low.shape[0] // (row_parts * mp_parts)
    count = reduce_count(row_parts, mp_parts)
    return pl.pallas_call(
        sum_low_kernel,
        out_shape=jax.ShapeDtypeStruct(low.shape, low.dtype),
        in_specs=[VMEM],
        out_specs=VMEM,
        scratch_shapes=[
            pltpu.VMEM(low.shape, low.dtype),
            pltpu.VMEM((reduce_sizes(piece, row_parts, mp_parts), BLOCK), low.dtype),
            pltpu.SemaphoreType.DMA((count,)),
            pltpu.SemaphoreType.DMA((count,)),
        ],
        compiler_params=pltpu.CompilerParams(
            collective_id=1, has_side_effects=True, vmem_limit_bytes=16 * MIB
        ),
    )(low)


def scatter_steps(links, src, acc, recv, out):
    m, mp_parts = lax.axis_index("mp"), lax.axis_size("mp")
    stages = []
    size, base, off = mp_parts, 0, 0
    depth = bits_of(mp_parts)
    for k in range(depth):
        size //= 2
        bit = (m // 2**k) % 2
        keep, send = base + bit * size, base + (1 - bit) * size
        source = src if k == 0 else acc
        copy = links.copy(
            source.at[pl.ds(send, size)], recv.at[pl.ds(off, size)], {"mp": flip(m, k)}
        )

        def merge(source=source, keep=keep, off=off, size=size, k=k):
            for t in range(size):
                a = source[keep + t].astype(jnp.float32)
                b = recv[off + t].astype(jnp.float32)
                if k == depth - 1:
                    out[...] = a + b
                else:
                    acc[keep + t] = (a + b).astype(acc.dtype)

        stages.append(([copy], merge))
        base, off = keep, off + size
    return stages


def sum_outputs_kernel(
    y_ref, sel_ref, own_ref, all_ref, y_acc, y_recv, acc_ref, recv_ref, send_sem, recv_sem
):
    greet(everyone())
    links = Links(send_sem, recv_sem)
    piece = sel_ref.shape[0] // (lax.axis_size("rows") * lax.axis_size("mp"))
    run_steps(
        steps_of(reduce_steps(links, sel_ref, acc_ref, recv_ref, all_ref, piece)),
        steps_of(scatter_steps(links, y_ref, y_acc, y_recv, own_ref)),
    )


def sum_outputs(y, selected):
    row_parts, mp_parts = lax.axis_size("rows"), lax.axis_size("mp")
    piece = selected.shape[0] // (row_parts * mp_parts)
    count = reduce_count(row_parts, mp_parts) + bits_of(mp_parts)
    _, tokens, part = y.shape
    return pl.pallas_call(
        sum_outputs_kernel,
        out_shape=(
            jax.ShapeDtypeStruct((tokens, part), jnp.float32),
            jax.ShapeDtypeStruct(selected.shape, selected.dtype),
        ),
        in_specs=[VMEM, VMEM],
        out_specs=(VMEM, VMEM),
        scratch_shapes=[
            pltpu.VMEM(y.shape, y.dtype),
            pltpu.VMEM((mp_parts - 1, tokens, part), y.dtype),
            pltpu.VMEM(selected.shape, selected.dtype),
            pltpu.VMEM((reduce_sizes(piece, row_parts, mp_parts), BLOCK), selected.dtype),
            pltpu.SemaphoreType.DMA((count,)),
            pltpu.SemaphoreType.DMA((count,)),
        ],
        compiler_params=pltpu.CompilerParams(
            collective_id=2, has_side_effects=True, vmem_limit_bytes=32 * MIB
        ),
    )(y, selected)


def pick_columns_kernel(places_ref, factor_ref, columns_ref, low_ref):
    j = pl.program_id(0)
    count = places_ref.shape[1]
    used = count * (count + 1) // 2 * BLOCK
    mp_parts = lax.axis_size("mp")
    part = factor_ref.shape[0] // mp_parts
    own = places_ref[1, j] != 0
    for at in range(mp_parts):
        q = reversed_bits(at, mp_parts)
        value = factor_ref[q * part : (q + 1) * part, :]
        columns_ref[at * part : (at + 1) * part, :] = jnp.where(own, value, 0.0)
    if low_ref.shape[0] > used:
        low_ref[used:, :] = jnp.zeros((low_ref.shape[0] - used, BLOCK), low_ref.dtype)
    for i in range(count):

        @pl.when(i >= j)
        def _():
            rows = pl.ds(pl.multiple_of(places_ref[2, i] * BLOCK, BLOCK), BLOCK)
            to = pl.ds(pl.multiple_of((i * (i + 1) // 2 + j) * BLOCK, BLOCK), BLOCK)
            both = (places_ref[3, i] != 0) & own
            low_ref[to, :] = jnp.where(both, factor_ref[rows, :], 0.0)


def padded(used):
    pieces = lax.axis_size("rows") * lax.axis_size("mp")
    return -(-used // (pieces * 16)) * pieces * 16


def pick_columns(places, factor):
    count = places.shape[1]
    rows = factor.shape[0]
    low_rows = padded(count * (count + 1) // 2 * BLOCK)
    return pl.pallas_call(
        pick_columns_kernel,
        out_shape=(
            jax.ShapeDtypeStruct((rows, count * BLOCK), jnp.float32),
            jax.ShapeDtypeStruct((low_rows, BLOCK), jnp.float32),
        ),
        grid_spec=pltpu.PrefetchScalarGridSpec(
            num_scalar_prefetch=1,
            grid=(count,),
            in_specs=[pl.BlockSpec((rows, BLOCK), lambda j, places: (0, places[0, j]))],
            out_specs=(
                pl.BlockSpec((rows, BLOCK), lambda j, places: (0, j)),
                pl.BlockSpec((low_rows, BLOCK), lambda j, places: (0, 0)),
            ),
        ),
    )(places, factor)


def pick_rows_kernel(places_ref, weight_ref, out_ref):
    inside = places_ref[3, pl.program_id(0)] != 0
    value = weight_ref[...].astype(jnp.float32)
    out_ref[...] = jnp.where(inside, value, 0.0).astype(jnp.bfloat16)


def pick_rows(places, weight):
    count = places.shape[1]
    width = weight.shape[1]
    return pl.pallas_call(
        pick_rows_kernel,
        out_shape=jax.ShapeDtypeStruct((count * BLOCK, width), jnp.bfloat16),
        grid_spec=pltpu.PrefetchScalarGridSpec(
            num_scalar_prefetch=1,
            grid=(count,),
            in_specs=[pl.BlockSpec((BLOCK, width), lambda i, places: (places[2, i], 0))],
            out_specs=pl.BlockSpec((BLOCK, width), lambda i, places: (i, 0)),
        ),
    )(places, weight)


def project_kernel(scale, places_ref, calib_ref, weight_ref, y_ref, sel_ref):
    step = pl.program_id(0)
    count = places_ref.shape[1]
    tokens = calib_ref.shape[0]
    tile = weight_ref.shape[0]
    part = y_ref.shape[2]

    @pl.when(step == 0)
    def _():
        sel_ref[...] = jnp.zeros(sel_ref.shape, sel_ref.dtype)

    value = lax.dot_general(
        calib_ref[...],
        weight_ref[...],
        (((1,), (1,)), ((), ())),
        preferred_element_type=jnp.float32,
    )
    value = (value * scale).astype(jnp.bfloat16)
    for s in range(tile // part):
        y_ref[s] = value[:, s * part : (s + 1) * part]
    for i in range(count):
        for s in range(tile // BLOCK):
            here = step * (tile // BLOCK) + s

            @pl.when((places_ref[3, i] != 0) & (places_ref[2, i] == here))
            def _():
                sel_ref[i * tokens : (i + 1) * tokens, :] = value[:, s * BLOCK : (s + 1) * BLOCK]


def project(places, calib, weight, scale):
    count = places.shape[1]
    tokens, width = calib.shape
    rows = weight.shape[0]
    mp_parts = lax.axis_size("mp")
    part = rows // mp_parts
    tile = max(part, BLOCK)
    sel_rows = padded(count * tokens)
    return pl.pallas_call(
        functools.partial(project_kernel, scale),
        out_shape=(
            jax.ShapeDtypeStruct((mp_parts, tokens, part), jnp.bfloat16),
            jax.ShapeDtypeStruct((sel_rows, BLOCK), jnp.bfloat16),
        ),
        grid_spec=pltpu.PrefetchScalarGridSpec(
            num_scalar_prefetch=1,
            grid=(rows // tile,),
            in_specs=[
                pl.BlockSpec((tokens, width), lambda i, places: (0, 0)),
                pl.BlockSpec((tile, width), lambda i, places: (i, 0)),
            ],
            out_specs=(
                pl.BlockSpec((tile // part, tokens, part), lambda i, places: (i, 0, 0)),
                pl.BlockSpec((sel_rows, BLOCK), lambda i, places: (0, 0)),
            ),
        ),
        compiler_params=pltpu.CompilerParams(vmem_limit_bytes=32 * MIB),
    )(places, calib, weight)


def invert(low_ref, out_ref, neg_ref, rhs_ref, pivot_ref):
    count = out_ref.shape[0] // BLOCK
    at = 0
    for i in range(count):
        for j in range(i + 1):
            block = low_ref[at : at + BLOCK, :]
            at += BLOCK
            out_ref[i * BLOCK : (i + 1) * BLOCK, j * BLOCK : (j + 1) * BLOCK] = block
            if j < i:
                out_ref[j * BLOCK : (j + 1) * BLOCK, i * BLOCK : (i + 1) * BLOCK] = block.T

    def stage(k, carry):
        here = pl.ds(pl.multiple_of(k * BLOCK, BLOCK), BLOCK)
        diag = out_ref[here, here]
        tiles = [diag[t * SUB : (t + 1) * SUB, :] for t in range(BLOCK // SUB)]
        tiles = sweep_block(tiles)
        for t in range(BLOCK // SUB):
            neg_ref[t * SUB : (t + 1) * SUB, :] = tiles[t]
        neg = neg_ref[...]
        r1, r2, r3 = split3(out_ref[here, :])
        a1, a2, a3 = split3(-neg)
        pivot_ref[...] = jnp.dot(
            jnp.concatenate([a1, a1, a2, a2, a1, a3], axis=1),
            jnp.concatenate([r1, r2, r1, r2, r3, r1], axis=0),
            preferred_element_type=jnp.float32,
        )
        pivot_ref[:, here] = neg
        b1, b2, b3 = split3(pivot_ref[...])
        for slot, part in enumerate((b1, b2, b1, b2, b3, b1)):
            rhs_ref[slot * BLOCK : (slot + 1) * BLOCK, :] = part

        def update(i, inner):
            rows = pl.ds(pl.multiple_of(i * BLOCK, BLOCK), BLOCK)
            c1, c2, c3 = split3(out_ref[rows, here])
            out_ref[rows, here] = jnp.zeros((BLOCK, BLOCK), jnp.float32)
            out_ref[rows, :] -= jnp.dot(
                jnp.concatenate([c1, c1, c2, c2, c1, c3], axis=1),
                rhs_ref[...],
                preferred_element_type=jnp.float32,
            )
            return inner

        lax.fori_loop(0, count, update, 0)
        out_ref[here, :] = pivot_ref[...]
        return carry

    lax.fori_loop(0, count, stage, 0)


def outputs_from(square_ref, columns_ref, y_ref, sel_ref, keep_ref, total_ref, factor_ref, out_ref):
    count = square_ref.shape[0] // BLOCK
    tokens = y_ref.shape[0]
    total_ref[...] = jnp.zeros(total_ref.shape, jnp.float32)

    def body(k, carry):
        here = pl.ds(pl.multiple_of(k * BLOCK, BLOCK), BLOCK)
        c1, c2, c3 = split3(columns_ref[:, here])
        n1, n2, n3 = split3(square_ref[here, :])
        total_ref[...] -= jnp.dot(
            jnp.concatenate([c1, c1, c2, c2, c1, c3], axis=1),
            jnp.concatenate([n1, n2, n1, n2, n3, n1], axis=0),
            preferred_element_type=jnp.float32,
        )
        return carry

    lax.fori_loop(0, count, body, 0)
    factor_ref[...] = total_ref[...].astype(jnp.bfloat16)
    selected = jnp.concatenate(
        [sel_ref[i * tokens : (i + 1) * tokens, :] for i in range(count)], axis=1
    )
    update = lax.dot_general(
        selected, factor_ref[...], (((1,), (1,)), ((), ())), preferred_element_type=jnp.float32
    )
    value = jnp.where(keep_ref[...] != 0.0, y_ref[...] - update, 0.0)
    out_ref[...] = value.astype(jnp.bfloat16)


def solve_kernel(
    low_ref, columns_ref, y_ref, sel_ref, keep_ref, factor_ref, out_ref,
    square_ref, neg_ref, rhs_ref, pivot_ref, total_ref,
):
    invert(low_ref, square_ref, neg_ref, rhs_ref, pivot_ref)
    outputs_from(
        square_ref, columns_ref, y_ref, sel_ref, keep_ref, total_ref, factor_ref, out_ref
    )


def solve(low, own_columns, own_y, selected, keep):
    part, order = own_columns.shape
    tokens = own_y.shape[0]
    return pl.pallas_call(
        solve_kernel,
        out_shape=(
            jax.ShapeDtypeStruct((part, order), jnp.bfloat16),
            jax.ShapeDtypeStruct((tokens, part), jnp.bfloat16),
        ),
        in_specs=[VMEM] * 5,
        out_specs=(VMEM, VMEM),
        scratch_shapes=[
            pltpu.VMEM((order, order), jnp.float32),
            pltpu.VMEM((BLOCK, BLOCK), jnp.float32),
            pltpu.VMEM((6 * BLOCK, order), jnp.bfloat16),
            pltpu.VMEM((BLOCK, order), jnp.float32),
            pltpu.VMEM((part, order), jnp.float32),
        ],
        compiler_params=pltpu.CompilerParams(vmem_limit_bytes=40 * MIB),
        cost_estimate=pl.CostEstimate(
            flops=60_000_000_000, bytes_accessed=2 * order * order * 4, transcendentals=0
        ),
    )(low, own_columns, own_y, selected, keep)


def moved_to(r, m, row_parts, mp_parts):
    per = row_parts // mp_parts
    return ((m + 1) % mp_parts) * per + r % per, r // per


def right_orders(row_parts):
    count = bits_of(row_parts)
    first = list(range(count))
    second = [1, 0] + first[2:] if count > 1 else first
    return first, second


def exchange_kernel(out_ref, factor_ref, left_ref, right_ref, all_factor_ref, send_sem, recv_sem):
    row_parts, mp_parts = lax.axis_size("rows"), lax.axis_size("mp")
    r, m = lax.axis_index("rows"), lax.axis_index("mp")
    per = row_parts // mp_parts
    tokens = out_ref.shape[0]
    to_row, to_mp = moved_to(r, m, row_parts, mp_parts)
    from_row = m * per + r % per
    from_mp = lax.rem(r // per + mp_parts - 1, mp_parts)
    devices = [{"mp": flip(m, k)} for k in range(bits_of(mp_parts))]
    devices += [{"rows": flip(r, k)} for k in range(bits_of(row_parts))]
    target = {"rows": to_row, "mp": to_mp}
    devices += [target, {"rows": from_row, "mp": from_mp}]
    greet(devices)
    links = Links(send_sem, recv_sem)
    mine = reversed_bits(m, mp_parts)

    orders = right_orders(row_parts)
    lists = []
    for h, order in enumerate(orders):
        half = tokens // 2
        slot = ordered_bits(to_row, order)
        copy = links.copy(
            out_ref.at[pl.ds(h * half, half)], right_ref.at[h, slot], target
        )
        stages = [([copy], None)]
        base, size = ordered_bits(r, order), 1
        for k in reversed(order):
            region = right_ref.at[h, pl.ds(base, size)]
            stages.append(([links.copy(region, region, {"rows": flip(r, k)})], None))
            base = base - ((base // size) % 2) * size
            size *= 2
        lists.append(steps_of(stages))
    for src, dst in ((out_ref, left_ref), (factor_ref, all_factor_ref)):
        stages = []
        base, size = mine, 1
        for k in reversed(range(bits_of(mp_parts))):
            region = dst.at[pl.ds(base, size)]
            source = src if size == 1 else region
            sink = dst.at[base] if size == 1 else region
            stages.append(([links.copy(source, sink, {"mp": flip(m, k)})], None))
            base = base - ((base // size) % 2) * size
            size *= 2
        lists.append(steps_of(stages))
    left_ref[mine] = out_ref[...]
    all_factor_ref[mine] = factor_ref[...]
    run_steps(*lists)


def exchange(outputs, factor):
    row_parts, mp_parts = lax.axis_size("rows"), lax.axis_size("mp")
    tokens, part = outputs.shape
    order = factor.shape[1]
    count = 2 * (1 + bits_of(row_parts)) + 2 * bits_of(mp_parts)
    return pl.pallas_call(
        exchange_kernel,
        out_shape=(
            jax.ShapeDtypeStruct((mp_parts, tokens, part), jnp.bfloat16),
            jax.ShapeDtypeStruct((2, row_parts, tokens // 2, part), jnp.bfloat16),
            jax.ShapeDtypeStruct((mp_parts, part, order), jnp.bfloat16),
        ),
        in_specs=[VMEM, VMEM],
        out_specs=(VMEM, VMEM, VMEM),
        scratch_shapes=[
            pltpu.SemaphoreType.DMA((count,)),
            pltpu.SemaphoreType.DMA((count,)),
        ],
        compiler_params=pltpu.CompilerParams(
            collective_id=3, has_side_effects=True, vmem_limit_bytes=32 * MIB
        ),
    )(outputs, factor)


def gram_kernel(row_parts, mp_parts, left_ref, right_ref, out_ref):
    per = row_parts // mp_parts
    tokens, part = left_ref.shape[1:]
    first, second = right_orders(row_parts)
    left = left_ref[0]
    for at in range(row_parts):
        source_mp = (at // per - 1) % mp_parts
        column = (at % per) * mp_parts + reversed_bits(source_mp, mp_parts)
        right = jnp.concatenate(
            [right_ref[0, ordered_bits(at, first)], right_ref[1, ordered_bits(at, second)]], axis=0
        )
        value = lax.dot_general(
            left, right, (((0,), (0,)), ((), ())), preferred_element_type=jnp.float32
        )
        out_ref[:, column * part : (column + 1) * part] = value / tokens


def gram_of(left, right):
    mp_parts, tokens, part = left.shape
    row_parts = right.shape[1]
    width = row_parts * part
    return pl.pallas_call(
        functools.partial(gram_kernel, row_parts, mp_parts),
        grid=(mp_parts,),
        in_specs=[pl.BlockSpec((1, tokens, part), lambda i: (i, 0, 0)), VMEM],
        out_specs=pl.BlockSpec((part, width), lambda i: (i, 0)),
        out_shape=jax.ShapeDtypeStruct((mp_parts * part, width), jnp.float32),
        compiler_params=pltpu.CompilerParams(vmem_limit_bytes=32 * MIB),
    )(left, right)


def prune_kernel(flags_ref, weight_ref, factor_ref, kept_ref, out_ref):
    step = pl.program_id(0)
    tile, width = weight_ref.shape
    chunk = min(width, 512)
    for c in range(width // chunk):
        lanes = slice(c * chunk, (c + 1) * chunk)
        update = jnp.dot(factor_ref[...], kept_ref[:, lanes], preferred_element_type=jnp.float32)
        value = weight_ref[:, lanes].astype(jnp.float32) - update
        for s in range(tile // BLOCK):
            gone = flags_ref[step * (tile // BLOCK) + s] != 0
            rows = slice(s * BLOCK, (s + 1) * BLOCK)
            out_ref[rows, lanes] = jnp.where(gone, 0.0, value[rows, :]).astype(jnp.bfloat16)


def prune(flags, weight, factor, kept_rows):
    rows, width = weight.shape
    order = factor.shape[1]
    tile = min(rows, 256)
    return pl.pallas_call(
        prune_kernel,
        out_shape=jax.ShapeDtypeStruct((rows, width), jnp.bfloat16),
        grid_spec=pltpu.PrefetchScalarGridSpec(
            num_scalar_prefetch=1,
            grid=(rows // tile,),
            in_specs=[
                pl.BlockSpec((tile, width), lambda i, flags: (i, 0)),
                pl.BlockSpec((tile, order), lambda i, flags: (i, 0)),
                pl.BlockSpec((order, width), lambda i, flags: (0, 0)),
            ],
            out_specs=pl.BlockSpec((tile, width), lambda i, flags: (i, 0)),
        ),
        compiler_params=pltpu.CompilerParams(vmem_limit_bytes=32 * MIB),
    )(flags, weight, factor, kept_rows)


def shards(calib, weight, inverse_factor, pruned_blocks):
    rows_dev, width_dev = weight.shape
    mp_parts = lax.axis_size("mp")
    full_width = width_dev * mp_parts
    part = rows_dev // mp_parts
    m = lax.axis_index("mp")
    row_start = lax.axis_index("rows") * rows_dev
    col_start = m * width_dev
    starts = pruned_blocks * BLOCK
    col_offsets = starts - col_start
    row_offsets = starts - row_start
    places = jnp.stack(
        [
            jnp.clip(col_offsets, 0, width_dev - BLOCK) // BLOCK,
            ((col_offsets >= 0) & (col_offsets < width_dev)).astype(jnp.int32),
            jnp.clip(row_offsets, 0, rows_dev - BLOCK) // BLOCK,
            ((row_offsets >= 0) & (row_offsets < rows_dev)).astype(jnp.int32),
        ]
    ).astype(jnp.int32)
    block_ids = row_start // BLOCK + jnp.arange(rows_dev // BLOCK, dtype=jnp.int32)
    flags = jnp.any(block_ids[:, None] == pruned_blocks[None, :], axis=1).astype(jnp.int32)
    own_start = row_start + reversed_bits(m, mp_parts) * part
    own_ids = (own_start + jnp.arange(part, dtype=jnp.int32)) // BLOCK
    keep = 1.0 - jnp.any(own_ids[:, None] == pruned_blocks[None, :], axis=1).astype(jnp.float32)

    columns, own_low = pick_columns(places, inverse_factor)
    own_kept = pick_rows(places, weight)
    kept_rows = lax.psum(own_kept, "rows")
    all_calib = lax.all_gather(calib, "rows", axis=0, tiled=True)
    own_columns = lax.psum_scatter(columns, "mp", scatter_dimension=0, tiled=True)
    low = sum_low(own_low)
    y, own_selected = project(places, all_calib, weight, float(full_width) ** (-0.5))
    own_y, selected = sum_outputs(y, own_selected)
    factor, outputs = solve(low, own_columns, own_y, selected, keep[None, :])
    left, right, all_factor = exchange(outputs, factor)
    gram_block = gram_of(left, right)
    pruned_weight = prune(
        flags, weight, all_factor.reshape(rows_dev, factor.shape[1]), kept_rows
    )
    return (pruned_weight, gram_block)


def solution(mesh):
    return jax.shard_map(
        shards,
        mesh=mesh,
        in_specs=(P("rows", "mp"), P("rows", "mp"), P("rows", "mp"), P()),
        out_specs=(P("rows", "mp"), P("rows", "mp")),
        check_vma=False,
    )
```

time: 437 us -> 284 us (0.65)
  waiting for transfers between devices: 309 us -> 0.74 us
  Pallas kernels: 86.1 us -> 253 us
  matrix products: 17.2 us -> 0 us
  local copies, waits for them, and re-layouts: 4.21 us -> 11.6 us
    pallas_call x2 -> x7, Pallas kernels: 71.7 us -> 241 us  [the longest x1 67.6 us: sum_low(): pl.pallas_call(sum_low_kernel, out_shape=jax.ShapeDtypeStruct(low.shape,...]
    psum x1 -> x0, waiting for transfers between devices: 139 us -> none  [shards(): low = lax.psum(own_low, ('rows', 'mp'))]
    all_gather x3 -> x0, waiting for transfers between devices: 73.9 us -> none  [the longest x1 53.9 us: shards(): right = lax.all_gather(moved, 'rows', axis=0, tiled=False)]
    psum x1, waiting for transfers between devices: 71.2 us -> 0.01 us  [shards(): kept_rows = lax.psum(own_kept, 'rows')]
    reduce_scatter x1 -> x0, waiting for transfers between devices: 23.9 us -> none  [shards(): lax.psum_scatter((partial_value * out_scale).astype(jnp.bfloat16), 'mp',...]
    dot_general x3 -> x0, matrix products: 17.2 us -> none  [the longest x1 8.35 us: shards(): lax.dot_general(factors, kept_rows, (((1,), (0,)), ((), ())), preferred_e...]
    unnamed x10 -> x20, local copies, waits for them, and re-layouts: 4.21 us -> 11.6 us
  transfers between devices with their start and end apart: 9 -> 3, of which waited for: 5 -> 0; matrix products, arithmetic and copies ran while one was open for 1% -> 1% of each run, Pallas kernels for 16% -> 87%
where the time goes in v1:
time: 284 us; the launch traced here: 283 us
  Pallas kernels  253 us (89%)
  between operations  15.6 us (5%)
  local copies, waits for them, and re-layouts  11.6 us (4%)
    pallas_call x1, Pallas kernels, sum_low(): pl.pallas_call(sum_low_kernel, out_shape=jax.ShapeDtypeStruct(low.shape,...  67.6 us
    pallas_call x1, Pallas kernels, solve(): pl.pallas_call(solve_kernel, out_shape=(jax.ShapeDtypeStruct((part, order...  67.3 us
    pallas_call x1, Pallas kernels, exchange(): pl.pallas_call(exchange_kernel, out_shape=(jax.ShapeDtypeStruct((mp_parts...  52.2 us
    pallas_call x1, Pallas kernels, sum_outputs(): pl.pallas_call(sum_outputs_kernel, out_shape=(jax.ShapeDtypeStruct((token...  38.5 us
    unnamed x20, local copies, waits for them, and re-layouts  11.6 us
    pallas_call x1, Pallas kernels, prune(): pl.pallas_call(prune_kernel, out_shape=jax.ShapeDtypeStruct((rows, width)...  6.74 us
    pallas_call x1, Pallas kernels, pick_columns(): pl.pallas_call(pick_columns_kernel, out_shape=(jax.ShapeDtypeStruct((rows...  6.1 us
  transfers between devices with their start and end apart: 3, of which 0 were waited for; matrix products, arithmetic and copies ran while one was open for 1% of the time, Pallas kernels for 87%

profile of v1, /device:TPU:0, one launch (start us, length us, event | category | flops | bytes accessed | tf_op | source)
XLA Modules:
  0.0 283.1 jit_solution(18402264483766758662)
XLA Ops:
  8.0 0.7 all-gather.2.cloned.1.call-update
  8.7 0.0 reduce-scatter.2.cloned.1.call-start
  8.8 0.7 fusion
  9.5 0.7 fusion.3
  10.1 0.6 pad_add_fusion.places_ref
  10.7 6.1 %shard_map.59 = (f32[1024,896]{1,0:T(8,128)}, f32[3584,128]{1,0:T(8,128)}) custom-call(s32[4,7]{1,0:T(4,128)} %pad_add_fusion.places_ref, f32[1024,2048]{1,0:T(8,128)} %factor_ref.1), custom_call_target="tpu_custom_call" | custom-call | tf_op jit(solution)/shard_map/pallas_call | solution.py:364
  16.9 5.3 %shard_map.65 = bf16[896,2048]{1,0:T(8,128)(2,1)} custom-call(s32[4,7]{1,0:T(4,128)} %pad_add_fusion.places_ref, bf16[1024,2048]{1,0:T(8,128)(2,1)} %weight_ref.5), custom_call_target="tpu_custom_call" | custom-call | tf_op jit(solution)/shard_map/pallas_call | solution.py:391
  22.2 0.6 copy-done.9
  22.8 0.2 compare_reduce_fusion.1
  23.0 0.1 compare_reduce_fusion
  23.1 0.6 copy-done.4
  23.7 67.6 %shard_map.60.low_ref = f32[3584,128]{1,0:T(8,128)S(1)} custom-call(f32[3584,128]{1,0:T(8,128)S(1)} %copy-done.4), custom_call_target="tpu_custom_call" | custom-call | tf_op jit(solution)/shard_map/pallas_call | solution.py:248
  91.3 1.2 copy-done.5
  92.5 2.2 copy-done
  94.7 1.6 copy-done.3
  96.3 4.2 %shard_map.61 = (bf16[4,512,256]{2,1,0:T(8,128)(2,1)S(1)}, bf16[3584,128]{1,0:T(8,128)(2,1)S(1)}) custom-call(s32[4,7]{1,0:T(4,128)S(1)} %copy-done.7, bf16[512,2048]{1,0:T(8,128)(2,1)S(1)} %copy-done.3, bf16[1024,2048]{1,0:T(8,128)(2,1)S(1)} %copy-done), custom_call_target="tpu_custom_call" | custom-call | tf_op jit(solution)/shard_map/pallas_call | solution.py:440
  100.5 38.5 %shard_map.62 = (f32[512,256]{1,0:T(8,128)S(1)}, bf16[3584,128]{1,0:T(8,128)(2,1)S(1)}) custom-call(bf16[4,512,256]{2,1,0:T(8,128)(2,1)S(1)} %get-tuple-element.15.y_ref, bf16[3584,128]{1,0:T(8,128)(2,1)S(1)} %get-tuple-element.16.sel_ref), custom_call_target="tpu_custom_call" | custom-call | tf_op jit(solution)/shard_map/pallas_call | solution.py:310
  139.1 1.2 copy-done.8
  140.3 67.3 %shard_map.63 = (bf16[256,896]{1,0:T(8,128)(2,1)S(1)}, bf16[512,256]{1,0:T(8,128)(2,1)S(1)}) custom-call(f32[3584,128]{1,0:T(8,128)S(1)} %copy-done.6, f32[256,896]{1,0:T(8,128)S(1)} %copy-done.8, f32[512,256]{1,0:T(8,128)S(1)} %get-tuple-element.17.y_ref, bf16[3584,128]{1,0:T(8,128)(2,1)S(1)} %get-tuple-element.18.sel_ref, f32[1,256]{1,0:T(1,128)S(1)} %bitcast.11), custom_call_target="tpu_custom_call" | custom-call | flops 60000002048 | bytes 6422528 | tf_op jit(solution)/shard_map/pallas_call | solution.py:552
  207.6 52.2 %shard_map.64 = (bf16[4,512,256]{2,1,0:T(8,128)(2,1)S(1)}, bf16[2,8,256,256]{3,2,1,0:T(8,128)(2,1)S(1)}, bf16[4,256,896]{2,1,0:T(8,128)(2,1)S(1)}) custom-call(bf16[512,256]{1,0:T(8,128)(2,1)S(1)} %get-tuple-element.19.out_ref, bf16[256,896]{1,0:T(8,128)(2,1)S(1)} %get-tuple-element.20.factor_ref), custom_call_target="tpu_custom_call" | custom-call | tf_op jit(solution)/shard_map/pallas_call | solution.py:639
  259.8 4.9 %shard_map.67 = f32[1024,2048]{1,0:T(8,128)} custom-call(bf16[4,512,256]{2,1,0:T(8,128)(2,1)S(1)} %get-tuple-element.22.left_ref, bf16[2,8,256,256]{3,2,1,0:T(8,128)(2,1)S(1)} %get-tuple-element.23.right_ref), custom_call_target="tpu_custom_call" | custom-call | tf_op jit(solution)/shard_map/pallas_call | solution.py:679
  264.7 2.2 copy-done.1
  266.9 2.0 copy-done.2
  268.9 6.7 %shard_map.66 = bf16[1024,2048]{1,0:T(8,128)(2,1)} custom-call(s32[8]{0:T(128)S(1)} %convert_element_type.16.flags_ref, bf16[1024,2048]{1,0:T(8,128)(2,1)S(1)} %copy-done.1, bf16[1024,896]{1,0:T(8,128)(2,1)S(1)} %bitcast.10, bf16[896,2048]{1,0:T(8,128)(2,1)S(1)} %copy-done.2), custom_call_target="tpu_custom_call" | custom-call | tf_op jit(solution)/shard_map/pallas_call | solution.py:707
  (23 shorter events, 0.2 us)
Async XLA Ops:
  8.0 84.5 %all-gather.2.cloned.1.call-start = ((), (), s32[]{:S(2)}) async-start(), calls=%async_computation.2 | async-start | bytes 2359296 | tf_op jit(solution)/shard_map/all_gather | solution.py:752
  8.7 130.3 %reduce-scatter.2.cloned.1.call-start = ((), (), s32[]{:S(2)}) async-start(), calls=%async_computation.1 | async-start | bytes 4587520 | tf_op jit(solution)/shard_map/reduce_scatter | solution.py:753
  16.8 247.9 %all-reduce.2.cloned.1.call-start = ((), (), s32[]{:S(2)}) async-start(), calls=%async_computation.3 | async-start | bytes 7340032 | tf_op jit(solution)/shard_map/psum | solution.py:751
  22.1 0.7 copy-start.9
  22.1 1.5 copy-start.4
  22.1 70.4 %copy-start.7 = (s32[4,7]{1,0:T(4,128)S(1)}, s32[4,7]{1,0:T(4,128)}, u32[]{:S(2)}) copy-start(s32[4,7]{1,0:T(4,128)} %pad_add_fusion.places_ref) | copy-start | bytes 340
  91.3 1.2 copy-start.5
  92.5 2.2 copy-start
  94.7 1.6 copy-start.3
  96.3 42.7 %copy-start.6 = (f32[3584,128]{1,0:T(8,128)S(1)}, f32[3584,128]{1,0:T(8,128)}, u32[]{:S(2)}) copy-start(f32[3584,128]{1,0:T(8,128)} %copy-done.5) | copy-start | bytes 5505028
  139.1 1.2 copy-start.8
  264.7 2.2 copy-start.1
  266.9 2.0 copy-start.2
Sparse Core Ops, SparseCore 0:
  10.9 61.5 all-gather.1
  76.2 159.5 all-reduce.1
Sparse Core Ops, SparseCore 1:
  16.9 51.7 reduce-scatter.1

commit v2 on v1

--- a/solution.py
+++ b/solution.py
@@ -226,30 +226,118 @@
     return steps
 
 
-def run_steps(*lists):
-    for s in range(max(len(one) for one in lists)):
+def joined(*lists):
+    def step(s):
         for one in lists:
             if s < len(one):
                 one[s]()
 
-
-def sum_low_kernel(src_ref, out_ref, acc_ref, recv_ref, send_sem, recv_sem):
+    return [functools.partial(step, s) for s in range(max(len(one) for one in lists))]
+
+
+def spread(steps, gap):
+    wide = []
+    for step in steps:
+        wide += [step] + [lambda: None] * (gap - 1)
+    return wide[: len(wide) - gap + 1]
+
+
+def run_steps(*lists):
+    for step in joined(*lists):
+        step()
+
+
+def ring_place(r):
+    row_parts = lax.axis_size("rows")
+    return (1 - r % 2) * (r // 2) + (r % 2) * (row_parts - 1 - r // 2)
+
+
+def ring_member(place):
+    row_parts = lax.axis_size("rows")
+    place = lax.rem(place + 2 * row_parts, row_parts)
+    second = (2 * place) // row_parts
+    return (1 - second) * 2 * place + second * (2 * (row_parts - 1 - place) + 1)
+
+
+def ring_devices():
+    place = ring_place(lax.axis_index("rows"))
+    return [{"rows": ring_member(place + 1)}, {"rows": ring_member(place - 1)}]
+
+
+def ring_sum_stages(links, src, recv, acc, out, sign, lanes):
+    row_parts = lax.axis_size("rows")
+    place = ring_place(lax.axis_index("rows"))
+    to = {"rows": ring_member(place + sign)}
+    size = src.shape[0] // row_parts
+
+    def chunk(step):
+        at = lax.rem(place - sign * step + 2 * row_parts, row_parts)
+        return span(at * size, size, 16)
+
+    stages = []
+    for s in range(row_parts - 1):
+        source = src.at[chunk(0), lanes] if s == 0 else acc.at[s - 1]
+        last = s == row_parts - 2
+
+        def merge(s=s, last=last, rows=chunk(s + 1)):
+            value = src[rows, lanes] + recv[s]
+            if last:
+                out[rows, lanes] = value
+            else:
+                acc[s] = value
+
+        stages.append(([links.copy(source, recv.at[s], to)], merge))
+    for s in range(row_parts - 1):
+        piece = out.at[chunk(s - 1), lanes]
+        stages.append(([links.copy(piece, piece, to)], None))
+    return stages
+
+
+def ring_gather_stages(links, src, out, sign, hops):
+    row_parts = lax.axis_size("rows")
+    place = ring_place(lax.axis_index("rows"))
+    to = {"rows": ring_member(place + sign)}
+    size = src.shape[0]
+    stages = []
+    for s in range(hops):
+        at = lax.rem(place - sign * s + 2 * row_parts, row_parts)
+        piece = out.at[span(at * size, size, 16)]
+        stages.append(([links.copy(src if s == 0 else piece, piece, to)], None))
+    return stages
+
+
+def gather_kernel(
+    src_ref, calib_ref, out_ref, all_calib_ref, acc_ref, recv_ref, send_sem, recv_sem
+):
+    row_parts = lax.axis_size("rows")
     greet(everyone())
     links = Links(send_sem, recv_sem)
-    pieces = lax.axis_size("rows") * lax.axis_size("mp")
-    piece = src_ref.shape[0] // pieces
-    run_steps(steps_of(reduce_steps(links, src_ref, acc_ref, recv_ref, out_ref, piece)))
-
-
-def sum_low(low):
+    piece = src_ref.shape[0] // (row_parts * lax.axis_size("mp"))
+    steps = joined(
+        steps_of(reduce_steps(links, src_ref, acc_ref, recv_ref, out_ref, piece)),
+        steps_of(ring_gather_stages(links, calib_ref, all_calib_ref, 1, row_parts // 2)),
+        steps_of(ring_gather_stages(links, calib_ref, all_calib_ref, -1, row_parts // 2 - 1)),
+    )
+    steps[0]()
+    place = ring_place(lax.axis_index("rows"))
+    size = calib_ref.shape[0]
+    all_calib_ref[span(place * size, size, 16), :] = calib_ref[...]
+    for step in steps[1:]:
+        step()
+
+
+def gather(low, calib):
     row_parts, mp_parts = lax.axis_size("rows"), lax.axis_size("mp")
     piece = low.shape[0] // (row_parts * mp_parts)
-    count = reduce_count(row_parts, mp_parts)
+    count = reduce_count(row_parts, mp_parts) + row_parts - 1
     return pl.pallas_call(
-        sum_low_kernel,
-        out_shape=jax.ShapeDtypeStruct(low.shape, low.dtype),
-        in_specs=[VMEM],
-        out_specs=VMEM,
+        gather_kernel,
+        out_shape=(
+            jax.ShapeDtypeStruct(low.shape, low.dtype),
+            jax.ShapeDtypeStruct((calib.shape[0] * row_parts, calib.shape[1]), calib.dtype),
+        ),
+        in_specs=[VMEM, VMEM],
+        out_specs=(VMEM, VMEM),
         scratch_shapes=[
             pltpu.VMEM(low.shape, low.dtype),
             pltpu.VMEM((reduce_sizes(piece, row_parts, mp_parts), BLOCK), low.dtype),
@@ -257,9 +345,9 @@
             pltpu.SemaphoreType.DMA((count,)),
         ],
         compiler_params=pltpu.CompilerParams(
-            collective_id=1, has_side_effects=True, vmem_limit_bytes=16 * MIB
-        ),
-    )(low)
+            collective_id=1, has_side_effects=True, vmem_limit_bytes=24 * MIB
+        ),
+    )(low, calib)
 
 
 def scatter_steps(links, src, acc, recv, out):
@@ -290,56 +378,12 @@
     return stages
 
 
-def sum_outputs_kernel(
-    y_ref, sel_ref, own_ref, all_ref, y_acc, y_recv, acc_ref, recv_ref, send_sem, recv_sem
-):
-    greet(everyone())
-    links = Links(send_sem, recv_sem)
-    piece = sel_ref.shape[0] // (lax.axis_size("rows") * lax.axis_size("mp"))
-    run_steps(
-        steps_of(reduce_steps(links, sel_ref, acc_ref, recv_ref, all_ref, piece)),
-        steps_of(scatter_steps(links, y_ref, y_acc, y_recv, own_ref)),
-    )
-
-
-def sum_outputs(y, selected):
-    row_parts, mp_parts = lax.axis_size("rows"), lax.axis_size("mp")
-    piece = selected.shape[0] // (row_parts * mp_parts)
-    count = reduce_count(row_parts, mp_parts) + bits_of(mp_parts)
-    _, tokens, part = y.shape
-    return pl.pallas_call(
-        sum_outputs_kernel,
-        out_shape=(
-            jax.ShapeDtypeStruct((tokens, part), jnp.float32),
-            jax.ShapeDtypeStruct(selected.shape, selected.dtype),
-        ),
-        in_specs=[VMEM, VMEM],
-        out_specs=(VMEM, VMEM),
-        scratch_shapes=[
-            pltpu.VMEM(y.shape, y.dtype),
-            pltpu.VMEM((mp_parts - 1, tokens, part), y.dtype),
-            pltpu.VMEM(selected.shape, selected.dtype),
-            pltpu.VMEM((reduce_sizes(piece, row_parts, mp_parts), BLOCK), selected.dtype),
-            pltpu.SemaphoreType.DMA((count,)),
-            pltpu.SemaphoreType.DMA((count,)),
-        ],
-        compiler_params=pltpu.CompilerParams(
-            collective_id=2, has_side_effects=True, vmem_limit_bytes=32 * MIB
-        ),
-    )(y, selected)
-
-
 def pick_columns_kernel(places_ref, factor_ref, columns_ref, low_ref):
     j = pl.program_id(0)
     count = places_ref.shape[1]
     used = count * (count + 1) // 2 * BLOCK
-    mp_parts = lax.axis_size("mp")
-    part = factor_ref.shape[0] // mp_parts
     own = places_ref[1, j] != 0
-    for at in range(mp_parts):
-        q = reversed_bits(at, mp_parts)
-        value = factor_ref[q * part : (q + 1) * part, :]
-        columns_ref[at * part : (at + 1) * part, :] = jnp.where(own, value, 0.0)
+    columns_ref[...] = jnp.where(own, factor_ref[...], 0.0)
     if low_ref.shape[0] > used:
         low_ref[used:, :] = jnp.zeros((low_ref.shape[0] - used, BLOCK), low_ref.dtype)
     for i in range(count):
@@ -380,7 +424,9 @@
 
 
 def pick_rows_kernel(places_ref, weight_ref, out_ref):
-    inside = places_ref[3, pl.program_id(0)] != 0
+    step = pl.program_id(0)
+    count = places_ref.shape[1]
+    inside = (places_ref[3, jnp.minimum(step, count - 1)] != 0) & (step < count)
     value = weight_ref[...].astype(jnp.float32)
     out_ref[...] = jnp.where(inside, value, 0.0).astype(jnp.bfloat16)
 
@@ -388,13 +434,19 @@
 def pick_rows(places, weight):
     count = places.shape[1]
     width = weight.shape[1]
+    unit = 16 * lax.axis_size("rows")
+    blocks = -(-(-(-count * BLOCK // unit) * unit) // BLOCK)
     return pl.pallas_call(
         pick_rows_kernel,
-        out_shape=jax.ShapeDtypeStruct((count * BLOCK, width), jnp.bfloat16),
+        out_shape=jax.ShapeDtypeStruct((blocks * BLOCK, width), jnp.bfloat16),
         grid_spec=pltpu.PrefetchScalarGridSpec(
             num_scalar_prefetch=1,
-            grid=(count,),
-            in_specs=[pl.BlockSpec((BLOCK, width), lambda i, places: (places[2, i], 0))],
+            grid=(blocks,),
+            in_specs=[
+                pl.BlockSpec(
+                    (BLOCK, width), lambda i, places: (places[2, jnp.minimum(i, count - 1)], 0)
+                )
+            ],
             out_specs=pl.BlockSpec((BLOCK, width), lambda i, places: (i, 0)),
         ),
     )(places, weight)
@@ -459,7 +511,7 @@
     )(places, calib, weight)
 
 
-def invert(low_ref, out_ref, neg_ref, rhs_ref, pivot_ref):
+def invert(low_ref, out_ref, neg_ref, rhs_ref, pivot_ref, steps):
     count = out_ref.shape[0] // BLOCK
     at = 0
     for i in range(count):
@@ -471,12 +523,16 @@
                 out_ref[j * BLOCK : (j + 1) * BLOCK, i * BLOCK : (i + 1) * BLOCK] = block.T
 
     def stage(k, carry):
+        for s in range(0, min(2 * count, len(steps)), 2):
+            pl.when(2 * k == s)(steps[s])
         here = pl.ds(pl.multiple_of(k * BLOCK, BLOCK), BLOCK)
         diag = out_ref[here, here]
         tiles = [diag[t * SUB : (t + 1) * SUB, :] for t in range(BLOCK // SUB)]
         tiles = sweep_block(tiles)
         for t in range(BLOCK // SUB):
             neg_ref[t * SUB : (t + 1) * SUB, :] = tiles[t]
+        for s in range(1, min(2 * count, len(steps)), 2):
+            pl.when(2 * k + 1 == s)(steps[s])
         neg = neg_ref[...]
         r1, r2, r3 = split3(out_ref[here, :])
         a1, a2, a3 = split3(-neg)
@@ -506,6 +562,8 @@
         return carry
 
     lax.fori_loop(0, count, stage, 0)
+    for s in range(2 * count, len(steps)):
+        steps[s]()
 
 
 def outputs_from(square_ref, columns_ref, y_ref, sel_ref, keep_ref, total_ref, factor_ref, out_ref):
@@ -537,38 +595,84 @@
 
 
 def solve_kernel(
-    low_ref, columns_ref, y_ref, sel_ref, keep_ref, factor_ref, out_ref,
+    low_ref, columns_ref, y_ref, sel_ref, keep_ref, kept_ref,
+    factor_ref, out_ref, all_kept_ref,
     square_ref, neg_ref, rhs_ref, pivot_ref, total_ref,
+    own_columns_ref, c_acc, c_recv, own_ref, y_acc, y_recv, all_ref, acc_ref, recv_ref,
+    k_acc, k_recv, send_sem, recv_sem,
 ):
-    invert(low_ref, square_ref, neg_ref, rhs_ref, pivot_ref)
+    greet(everyone())
+    links = Links(send_sem, recv_sem)
+    piece = sel_ref.shape[0] // (lax.axis_size("rows") * lax.axis_size("mp"))
+    half = kept_ref.shape[1] // 2
+    sum_steps = joined(
+        steps_of(reduce_steps(links, sel_ref, acc_ref, recv_ref, all_ref, piece)),
+        steps_of(scatter_steps(links, y_ref, y_acc, y_recv, own_ref)),
+    )
+    steps = joined(
+        steps_of(
+            ring_sum_stages(
+                links, kept_ref, k_recv.at[0], k_acc.at[0], all_kept_ref, 1, slice(0, half)
+            )
+        ),
+        steps_of(
+            ring_sum_stages(
+                links, kept_ref, k_recv.at[1], k_acc.at[1], all_kept_ref, -1, slice(half, 2 * half)
+            )
+        ),
+        spread(sum_steps, 2),
+        spread(steps_of(scatter_steps(links, columns_ref, c_acc, c_recv, own_columns_ref)), 6),
+    )
+    invert(low_ref, square_ref, neg_ref, rhs_ref, pivot_ref, steps)
     outputs_from(
-        square_ref, columns_ref, y_ref, sel_ref, keep_ref, total_ref, factor_ref, out_ref
+        square_ref, own_columns_ref, own_ref, all_ref, keep_ref, total_ref, factor_ref, out_ref
     )
 
 
-def solve(low, own_columns, own_y, selected, keep):
-    part, order = own_columns.shape
-    tokens = own_y.shape[0]
+def solve(low, columns, y, selected, keep, kept):
+    row_parts, mp_parts = lax.axis_size("rows"), lax.axis_size("mp")
+    piece = selected.shape[0] // (row_parts * mp_parts)
+    copies = reduce_count(row_parts, mp_parts) + 2 * bits_of(mp_parts)
+    copies += 4 * (row_parts - 1)
+    chunk = (row_parts - 1, kept.shape[0] // row_parts, kept.shape[1] // 2)
+    _, part, order = columns.shape
+    tokens = y.shape[1]
     return pl.pallas_call(
         solve_kernel,
         out_shape=(
             jax.ShapeDtypeStruct((part, order), jnp.bfloat16),
             jax.ShapeDtypeStruct((tokens, part), jnp.bfloat16),
-        ),
-        in_specs=[VMEM] * 5,
-        out_specs=(VMEM, VMEM),
+            jax.ShapeDtypeStruct(kept.shape, kept.dtype),
+        ),
+        in_specs=[VMEM] * 6,
+        out_specs=(VMEM, VMEM, VMEM),
         scratch_shapes=[
             pltpu.VMEM((order, order), jnp.float32),
             pltpu.VMEM((BLOCK, BLOCK), jnp.float32),
             pltpu.VMEM((6 * BLOCK, order), jnp.bfloat16),
             pltpu.VMEM((BLOCK, order), jnp.float32),
             pltpu.VMEM((part, order), jnp.float32),
+            pltpu.VMEM((part, order), jnp.float32),
+            pltpu.VMEM(columns.shape, jnp.float32),
+            pltpu.VMEM((mp_parts - 1, part, order), jnp.float32),
+            pltpu.VMEM((tokens, part), jnp.float32),
+            pltpu.VMEM(y.shape, y.dtype),
+            pltpu.VMEM((mp_parts - 1, tokens, part), y.dtype),
+            pltpu.VMEM(selected.shape, selected.dtype),
+            pltpu.VMEM(selected.shape, selected.dtype),
+            pltpu.VMEM((reduce_sizes(piece, row_parts, mp_parts), BLOCK), selected.dtype),
+            pltpu.VMEM((2,) + chunk, kept.dtype),
+            pltpu.VMEM((2,) + chunk, kept.dtype),
+            pltpu.SemaphoreType.DMA((copies,)),
+            pltpu.SemaphoreType.DMA((copies,)),
         ],
-        compiler_params=pltpu.CompilerParams(vmem_limit_bytes=40 * MIB),
+        compiler_params=pltpu.CompilerParams(
+            collective_id=2, has_side_effects=True, vmem_limit_bytes=48 * MIB
+        ),
         cost_estimate=pl.CostEstimate(
             flops=60_000_000_000, bytes_accessed=2 * order * order * 4, transcendentals=0
         ),
-    )(low, own_columns, own_y, selected, keep)
+    )(low, columns, y, selected, keep, kept)
 
 
 def moved_to(r, m, row_parts, mp_parts):
@@ -746,15 +850,12 @@
     own_ids = (own_start + jnp.arange(part, dtype=jnp.int32)) // BLOCK
     keep = 1.0 - jnp.any(own_ids[:, None] == pruned_blocks[None, :], axis=1).astype(jnp.float32)
 
+    own_kept = pick_rows(places, weight)
     columns, own_low = pick_columns(places, inverse_factor)
-    own_kept = pick_rows(places, weight)
-    kept_rows = lax.psum(own_kept, "rows")
-    all_calib = lax.all_gather(calib, "rows", axis=0, tiled=True)
-    own_columns = lax.psum_scatter(columns, "mp", scatter_dimension=0, tiled=True)
-    low = sum_low(own_low)
+    columns = columns.reshape(mp_parts, part, columns.shape[1])
+    low, all_calib = gather(own_low, calib)
     y, own_selected = project(places, all_calib, weight, float(full_width) ** (-0.5))
-    own_y, selected = sum_outputs(y, own_selected)
-    factor, outputs = solve(low, own_columns, own_y, selected, keep[None, :])
+    factor, outputs, kept_rows = solve(low, columns, y, own_selected, keep[None, :], own_kept)
     left, right, all_factor = exchange(outputs, factor)
     gram_block = gram_of(left, right)
     pruned_weight = prune(

time: 284 us -> 251 us (0.88)
  between operations: 15.6 us -> 0.77 us
  Pallas kernels: 253 us -> 241 us
  local copies, waits for them, and re-layouts: 11.6 us -> 5.73 us
    pallas_call x3 -> x2, Pallas kernels: 111 us -> 63.9 us  [the longest x1 57.4 us: gather(): pl.pallas_call(gather_kernel, out_shape=(jax.ShapeDtypeStruct(low.shape,...]
    pallas_call x1, Pallas kernels: 67.3 us -> 110 us  [solve(): pl.pallas_call(solve_kernel, out_shape=(jax.ShapeDtypeStruct((part, order...]
    pallas_call x1, Pallas kernels: 52.2 us -> 43.8 us  [exchange(): pl.pallas_call(exchange_kernel, out_shape=(jax.ShapeDtypeStruct((mp_parts...]
    unnamed x20 -> x12, local copies, waits for them, and re-layouts: 11.6 us -> 5.73 us
  transfers between devices with their start and end apart: 3 -> 0, of which waited for: 0 -> 0; matrix products, arithmetic and copies ran while one was open for 1% -> 0% of each run, Pallas kernels for 87% -> 0%
where the time goes in v2:
time: 251 us
  Pallas kernels  241 us (96%)
  local copies, waits for them, and re-layouts  5.73 us (2%)
  other arithmetic  3.54 us (1%)
    pallas_call x1, Pallas kernels, solve(): pl.pallas_call(solve_kernel, out_shape=(jax.ShapeDtypeStruct((part, order...  110 us
    pallas_call x1, Pallas kernels, gather(): pl.pallas_call(gather_kernel, out_shape=(jax.ShapeDtypeStruct(low.shape,...  57.4 us
    pallas_call x1, Pallas kernels, exchange(): pl.pallas_call(exchange_kernel, out_shape=(jax.ShapeDtypeStruct((mp_parts...  43.8 us
    pallas_call x1, Pallas kernels, pick_columns(): pl.pallas_call(pick_columns_kernel, out_shape=(jax.ShapeDtypeStruct((rows...  7.39 us
    pallas_call x1, Pallas kernels, prune(): pl.pallas_call(prune_kernel, out_shape=jax.ShapeDtypeStruct((rows, width)...  6.64 us
    pallas_call x1, Pallas kernels, pick_rows(): pl.pallas_call(pick_rows_kernel, out_shape=jax.ShapeDtypeStruct((blocks *...  6.45 us
    unnamed x12, local copies, waits for them, and re-layouts  5.73 us

profile of v2, /device:TPU:0, one launch (start us, length us, event | category | flops | bytes accessed | tf_op | source)
XLA Modules:
  0.0 250.8 jit_solution(2114175995764032942)
XLA Ops:
  0.7 0.8 compare_reduce_fusion.1
  1.6 0.7 compare_reduce_fusion
  2.3 0.7 fusion
  3.0 0.7 fusion.3
  3.6 0.6 pad_add_fusion.places_ref
  4.2 6.4 %shard_map.62.kept_ref = bf16[896,2048]{1,0:T(8,128)(2,1)} custom-call(s32[4,7]{1,0:T(4,128)} %pad_add_fusion.places_ref, bf16[1024,2048]{1,0:T(8,128)(2,1)} %weight_ref.5), custom_call_target="tpu_custom_call" | custom-call | tf_op jit(solution)/shard_map/pallas_call | solution.py:439
  10.7 0.0 copy-start.4
  10.7 0.0 copy-start.5
  10.7 7.4 %shard_map.59 = (f32[1024,896]{1,0:T(8,128)}, f32[3584,128]{1,0:T(8,128)}) custom-call(s32[4,7]{1,0:T(4,128)} %pad_add_fusion.places_ref, f32[1024,2048]{1,0:T(8,128)} %factor_ref.1), custom_call_target="tpu_custom_call" | custom-call | tf_op jit(solution)/shard_map/pallas_call | solution.py:408
  18.1 0.0 copy-done.4
  18.1 1.5 copy-done.3
  19.6 57.4 %shard_map.60 = (f32[3584,128]{1,0:T(8,128)S(1)}, bf16[512,2048]{1,0:T(8,128)(2,1)S(1)}) custom-call(f32[3584,128]{1,0:T(8,128)S(1)} %copy-done.3, bf16[64,2048]{1,0:T(8,128)(2,1)S(1)} %copy-done.4), custom_call_target="tpu_custom_call" | custom-call | tf_op jit(solution)/shard_map/pallas_call | solution.py:333
  77.0 0.0 copy-done.5
  77.0 0.0 copy-start
  77.0 2.2 copy-done
  79.2 4.2 %shard_map.61 = (bf16[4,512,256]{2,1,0:T(8,128)(2,1)S(1)}, bf16[3584,128]{1,0:T(8,128)(2,1)S(1)}) custom-call(s32[4,7]{1,0:T(4,128)S(1)} %copy-done.5, bf16[512,2048]{1,0:T(8,128)(2,1)S(1)} %get-tuple-element.17.calib_ref, bf16[1024,2048]{1,0:T(8,128)(2,1)S(1)} %copy-done), custom_call_target="tpu_custom_call" | custom-call | tf_op jit(solution)/shard_map/pallas_call | solution.py:492
  83.4 0.0 copy-start.1
  83.4 110.0 %shard_map.63 = (bf16[256,896]{1,0:T(8,128)(2,1)S(1)}, bf16[512,256]{1,0:T(8,128)(2,1)S(1)}, bf16[896,2048]{1,0:T(8,128)(2,1)}) custom-call(f32[3584,128]{1,0:T(8,128)S(1)} %get-tuple-element.15.low_ref, f32[4,256,896]{2,1,0:T(8,128)} %bitcast.13, bf16[4,512,256]{2,1,0:T(8,128)(2,1)S(1)} %get-tuple-element.18.y_ref, ...), custom_call_target="tpu_custom_call" | custom-call | flops 60000002048 | bytes 6422528 | tf_op jit(solution)/shard_map/pallas_call | solution.py:640
  193.5 43.8 %shard_map.64 = (bf16[4,512,256]{2,1,0:T(8,128)(2,1)S(1)}, bf16[2,8,256,256]{3,2,1,0:T(8,128)(2,1)S(1)}, bf16[4,256,896]{2,1,0:T(8,128)(2,1)S(1)}) custom-call(bf16[512,256]{1,0:T(8,128)(2,1)S(1)} %get-tuple-element.20.out_ref, bf16[256,896]{1,0:T(8,128)(2,1)S(1)} %get-tuple-element.21.factor_ref), custom_call_target="tpu_custom_call" | custom-call | tf_op jit(solution)/shard_map/pallas_call | solution.py:743
  237.3 0.0 copy-done.1
  237.3 0.0 copy-start.2
  237.3 2.0 copy-done.2
  239.3 6.6 %shard_map.65 = bf16[1024,2048]{1,0:T(8,128)(2,1)} custom-call(s32[8]{0:T(128)S(1)} %convert_element_type.16.flags_ref, bf16[1024,2048]{1,0:T(8,128)(2,1)S(1)} %copy-done.1, bf16[1024,896]{1,0:T(8,128)(2,1)S(1)} %bitcast.11, bf16[896,2048]{1,0:T(8,128)(2,1)S(1)} %copy-done.2), custom_call_target="tpu_custom_call" | custom-call | tf_op jit(solution)/shard_map/pallas_call | solution.py:811
  246.0 4.9 %shard_map.66 = f32[1024,2048]{1,0:T(8,128)} custom-call(bf16[4,512,256]{2,1,0:T(8,128)(2,1)S(1)} %get-tuple-element.24.left_ref, bf16[2,8,256,256]{3,2,1,0:T(8,128)(2,1)S(1)} %get-tuple-element.25.right_ref), custom_call_target="tpu_custom_call" | custom-call | tf_op jit(solution)/shard_map/pallas_call | solution.py:783
  (5 shorter events, 0.0 us)
Async XLA Ops:
  10.7 7.4 %copy-start.4 = (bf16[64,2048]{1,0:T(8,128)(2,1)S(1)}, bf16[64,2048]{1,0:T(8,128)(2,1)}, u32[]{:S(2)}) copy-start(bf16[64,2048]{1,0:T(8,128)(2,1)} %calib_ref.1) | copy-start | bytes 786436
  10.7 66.3 %copy-start.5 = (s32[4,7]{1,0:T(4,128)S(1)}, s32[4,7]{1,0:T(4,128)}, u32[]{:S(2)}) copy-start(s32[4,7]{1,0:T(4,128)} %pad_add_fusion.places_ref) | copy-start | bytes 340
  18.1 1.5 copy-start.3
  77.0 2.2 copy-start
  83.4 153.9 %copy-start.1 = (bf16[1024,2048]{1,0:T(8,128)(2,1)S(1)}, bf16[1024,2048]{1,0:T(8,128)(2,1)}, u32[]{:S(2)}) copy-start(bf16[1024,2048]{1,0:T(8,128)(2,1)} %weight_ref.5) | copy-start | bytes 12582916
  237.3 2.0 copy-start.2

commit v3 on v2

--- a/solution.py
+++ b/solution.py
@@ -10,6 +10,7 @@
 BLOCK = 128
 SUB = 8
 GROUP = 4
+TICKS = 4
 MIB = 1024 * 1024
 VMEM = pl.BlockSpec(memory_space=pltpu.VMEM)
 SMEM = pl.BlockSpec(memory_space=pltpu.SMEM)
@@ -23,11 +24,13 @@
     return first, second, third
 
 
-def sweep_block(tiles):
+def sweep_block(tiles, between):
     lane = lax.broadcasted_iota(jnp.int32, (SUB, BLOCK), 1)
     sublane = lax.broadcasted_iota(jnp.int32, (SUB, BLOCK), 0)
     wide = (SUB, BLOCK)
     for p in range(0, BLOCK, GROUP):
+        if p == BLOCK // 2:
+            between()
         own, s = p // SUB, p % SUB
         rows = [
             jnp.broadcast_to(tiles[own][s + a : s + a + 1, :], wide) for a in range(GROUP)
@@ -132,80 +135,90 @@
     return devices
 
 
-def add_rows(out_ref, out_at, left_ref, left_at, right_ref, right_at, size, unit):
-    chunk = unit
-
-    def body(t, carry):
-        step = pl.multiple_of(t * chunk, chunk)
-        a = left_ref[span(left_at + step, chunk, 16), :].astype(jnp.float32)
-        b = right_ref[span(right_at + step, chunk, 16), :].astype(jnp.float32)
-        out_ref[span(out_at + step, chunk, 16), :] = (a + b).astype(out_ref.dtype)
-        return carry
-
-    lax.fori_loop(0, size // chunk, body, 0)
-
-
-def reduce_sizes(piece, row_parts, mp_parts):
-    size = piece * row_parts * mp_parts
-    return (size - piece * row_parts) + (row_parts - 1) * piece
-
-
-def reduce_count(row_parts, mp_parts):
-    return 2 * bits_of(mp_parts) + 2 * (row_parts - 1)
-
-
-def reduce_steps(links, src, acc, recv, out, piece):
+def reduce_plans(rows):
+    pieces = lax.axis_size("rows") * lax.axis_size("mp")
+    depth = bits_of(lax.axis_size("mp"))
+    units = rows // (16 * pieces)
+    first = max(1, min(units - 1, (2 * units + 1) // 3))
+    order = [f"mp{k}" for k in range(depth)]
+    plans = [(0, 16 * first, order + ["rows"])]
+    if units > first:
+        plans.append((16 * first * pieces, 16 * (units - first), order[:1] + ["rows"] + order[1:]))
+    return plans
+
+
+def reduce_sizes(rows):
+    row_parts, mp_parts = lax.axis_size("rows"), lax.axis_size("mp")
+    total = 0
+    for _, piece, order in reduce_plans(rows):
+        size = piece * row_parts * mp_parts
+        for dim in order:
+            parts = row_parts if dim == "rows" else 2
+            total += size - size // parts
+            size //= parts
+    return total
+
+
+def reduce_count():
+    return 4 * (bits_of(lax.axis_size("mp")) + lax.axis_size("rows") - 1)
+
+
+def reduce_lists(links, src, acc, recv, out):
+    lists, off = [], 0
+    for start, piece, order in reduce_plans(src.shape[0]):
+        stages, off = reduce_stages(links, src, acc, recv, out, start, piece, order, off)
+        lists.append(steps_of(stages))
+    return joined(*lists)
+
+
+def reduce_stages(links, src, acc, recv, out, start, piece, order, off):
     row_parts, mp_parts = lax.axis_size("rows"), lax.axis_size("mp")
     r, m = lax.axis_index("rows"), lax.axis_index("mp")
-    stages = []
-    size, base, off = piece * row_parts * mp_parts, 0, 0
-    held = []
-    for k in range(bits_of(mp_parts)):
-        held.append((base, size))
-        size //= 2
-        bit = (m // 2**k) % 2
-        keep, send = base + bit * size, base + (1 - bit) * size
-        source = src if k == 0 else acc
-        copy = links.copy(
-            source.at[span(send, size, 16)],
-            recv.at[pl.ds(off, size)],
-            {"mp": flip(m, k)},
-        )
-
-        def merge(source=source, keep=keep, off=off, size=size):
-            add_rows(acc, keep, source, keep, recv, off, size, piece)
-
-        stages.append(([copy], merge))
-        base, off = keep, off + size
-    copies = []
-    for d in range(1, row_parts):
-        to = lax.rem(r + d, row_parts)
-        copies.append(
-            links.copy(
-                acc.at[span(base + to * piece, piece, 16)],
-                recv.at[pl.ds(off + (d - 1) * piece, piece)],
-                {"rows": to},
+    stages, held = [], []
+    base, size = start, piece * row_parts * mp_parts
+    for at, dim in enumerate(order):
+        parts = row_parts if dim == "rows" else 2
+        k = None if dim == "rows" else int(dim[2:])
+        size //= parts
+        source = src if at == 0 else acc
+        sink = out if at == len(order) - 1 else acc
+        copies = []
+        for d in range(1, parts):
+            to = lax.rem(r + d, row_parts) if k is None else 1 - (m // 2**k) % 2
+            device = {"rows": to} if k is None else {"mp": flip(m, k)}
+            copies.append(
+                links.copy(
+                    source.at[span(base + to * size, size, 16)],
+                    recv.at[pl.ds(off + (d - 1) * size, size)],
+                    device,
+                )
             )
-        )
-
-    def total(base=base, off=off):
-        mine = span(base + r * piece, piece, 16)
-        value = acc[mine, :].astype(jnp.float32)
-        for d in range(1, row_parts):
-            value = value + recv[pl.ds(off + (d - 1) * piece, piece), :].astype(jnp.float32)
-        out[mine, :] = value.astype(out.dtype)
-
-    stages.append((copies, total))
-    copies = []
-    for d in range(1, row_parts):
-        mine = out.at[span(base + r * piece, piece, 16)]
-        copies.append(links.copy(mine, mine, {"rows": lax.rem(r + d, row_parts)}))
-    stages.append((copies, None))
-    for k in reversed(range(bits_of(mp_parts))):
-        mine = out.at[span(base, size, 16)]
-        stages.append(([links.copy(mine, mine, {"mp": flip(m, k)})], None))
-        base, size = held[k]
-    return stages
+        keep = base + (r if k is None else (m // 2**k) % 2) * size
+
+        def merge(source=source, sink=sink, keep=keep, off=off, size=size, parts=parts):
+            def body(t, carry):
+                step = pl.multiple_of(t * piece, 16)
+                value = source[span(keep + step, piece, 16), :].astype(jnp.float32)
+                for d in range(1, parts):
+                    landed = recv[span(off + (d - 1) * size + step, piece, 16), :]
+                    value = value + landed.astype(jnp.float32)
+                sink[span(keep + step, piece, 16), :] = value.astype(sink.dtype)
+                return carry
+
+            lax.fori_loop(0, size // piece, body, 0)
+
+        stages.append((copies, merge))
+        off += (parts - 1) * size
+        base = keep
+        held.append((dim, k, keep, size))
+    for dim, k, keep, size in reversed(held):
+        mine = out.at[span(keep, size, 16)]
+        if k is None:
+            devices = [{"rows": lax.rem(r + d, row_parts)} for d in range(1, row_parts)]
+        else:
+            devices = [{"mp": flip(m, k)}]
+        stages.append(([links.copy(mine, mine, device) for device in devices], None))
+    return stages, off
 
 
 def steps_of(stages):
@@ -312,9 +325,8 @@
     row_parts = lax.axis_size("rows")
     greet(everyone())
     links = Links(send_sem, recv_sem)
-    piece = src_ref.shape[0] // (row_parts * lax.axis_size("mp"))
     steps = joined(
-        steps_of(reduce_steps(links, src_ref, acc_ref, recv_ref, out_ref, piece)),
+        reduce_lists(links, src_ref, acc_ref, recv_ref, out_ref),
         steps_of(ring_gather_stages(links, calib_ref, all_calib_ref, 1, row_parts // 2)),
         steps_of(ring_gather_stages(links, calib_ref, all_calib_ref, -1, row_parts // 2 - 1)),
     )
@@ -327,9 +339,8 @@
 
 
 def gather(low, calib):
-    row_parts, mp_parts = lax.axis_size("rows"), lax.axis_size("mp")
-    piece = low.shape[0] // (row_parts * mp_parts)
-    count = reduce_count(row_parts, mp_parts) + row_parts - 1
+    row_parts = lax.axis_size("rows")
+    count = reduce_count() + row_parts - 1
     return pl.pallas_call(
         gather_kernel,
         out_shape=(
@@ -340,7 +351,7 @@
         out_specs=(VMEM, VMEM),
         scratch_shapes=[
             pltpu.VMEM(low.shape, low.dtype),
-            pltpu.VMEM((reduce_sizes(piece, row_parts, mp_parts), BLOCK), low.dtype),
+            pltpu.VMEM((reduce_sizes(low.shape[0]), BLOCK), low.dtype),
             pltpu.SemaphoreType.DMA((count,)),
             pltpu.SemaphoreType.DMA((count,)),
         ],
@@ -522,17 +533,19 @@
             if j < i:
                 out_ref[j * BLOCK : (j + 1) * BLOCK, i * BLOCK : (i + 1) * BLOCK] = block.T
 
+    def tick(k, at):
+        for s in range(at, min(TICKS * count, len(steps)), TICKS):
+            pl.when(TICKS * k + at == s)(steps[s])
+
     def stage(k, carry):
-        for s in range(0, min(2 * count, len(steps)), 2):
-            pl.when(2 * k == s)(steps[s])
+        tick(k, 0)
         here = pl.ds(pl.multiple_of(k * BLOCK, BLOCK), BLOCK)
         diag = out_ref[here, here]
         tiles = [diag[t * SUB : (t + 1) * SUB, :] for t in range(BLOCK // SUB)]
-        tiles = sweep_block(tiles)
+        tiles = sweep_block(tiles, lambda: tick(k, 1))
         for t in range(BLOCK // SUB):
             neg_ref[t * SUB : (t + 1) * SUB, :] = tiles[t]
-        for s in range(1, min(2 * count, len(steps)), 2):
-            pl.when(2 * k + 1 == s)(steps[s])
+        tick(k, 2)
         neg = neg_ref[...]
         r1, r2, r3 = split3(out_ref[here, :])
         a1, a2, a3 = split3(-neg)
@@ -557,12 +570,14 @@
             )
             return inner
 
-        lax.fori_loop(0, count, update, 0)
+        lax.fori_loop(0, count // 2, update, 0)
+        tick(k, 3)
+        lax.fori_loop(count // 2, count, update, 0)
         out_ref[here, :] = pivot_ref[...]
         return carry
 
     lax.fori_loop(0, count, stage, 0)
-    for s in range(2 * count, len(steps)):
+    for s in range(TICKS * count, len(steps)):
         steps[s]()
 
 
@@ -603,25 +618,27 @@
 ):
     greet(everyone())
     links = Links(send_sem, recv_sem)
-    piece = sel_ref.shape[0] // (lax.axis_size("rows") * lax.axis_size("mp"))
-    half = kept_ref.shape[1] // 2
     sum_steps = joined(
-        steps_of(reduce_steps(links, sel_ref, acc_ref, recv_ref, all_ref, piece)),
+        reduce_lists(links, sel_ref, acc_ref, recv_ref, all_ref),
         steps_of(scatter_steps(links, y_ref, y_acc, y_recv, own_ref)),
     )
+    lanes = kept_ref.shape[1] // 4
+    rings = []
+    for at in range(4):
+        stages = ring_sum_stages(
+            links,
+            kept_ref,
+            k_recv.at[at],
+            k_acc.at[at],
+            all_kept_ref,
+            1 - 2 * (at % 2),
+            slice(at * lanes, (at + 1) * lanes),
+        )
+        rings.append([lambda: None] * (at // 2) + spread(steps_of(stages), 2))
     steps = joined(
-        steps_of(
-            ring_sum_stages(
-                links, kept_ref, k_recv.at[0], k_acc.at[0], all_kept_ref, 1, slice(0, half)
-            )
-        ),
-        steps_of(
-            ring_sum_stages(
-                links, kept_ref, k_recv.at[1], k_acc.at[1], all_kept_ref, -1, slice(half, 2 * half)
-            )
-        ),
-        spread(sum_steps, 2),
-        spread(steps_of(scatter_steps(links, columns_ref, c_acc, c_recv, own_columns_ref)), 6),
+        *rings,
+        spread(sum_steps, TICKS),
+        spread(steps_of(scatter_steps(links, columns_ref, c_acc, c_recv, own_columns_ref)), 3 * TICKS),
     )
     invert(low_ref, square_ref, neg_ref, rhs_ref, pivot_ref, steps)
     outputs_from(
@@ -631,10 +648,9 @@
 
 def solve(low, columns, y, selected, keep, kept):
     row_parts, mp_parts = lax.axis_size("rows"), lax.axis_size("mp")
-    piece = selected.shape[0] // (row_parts * mp_parts)
-    copies = reduce_count(row_parts, mp_parts) + 2 * bits_of(mp_parts)
-    copies += 4 * (row_parts - 1)
-    chunk = (row_parts - 1, kept.shape[0] // row_parts, kept.shape[1] // 2)
+    copies = reduce_count() + 2 * bits_of(mp_parts)
+    copies += 8 * (row_parts - 1)
+    chunk = (row_parts - 1, kept.shape[0] // row_parts, kept.shape[1] // 4)
     _, part, order = columns.shape
     tokens = y.shape[1]
     return pl.pallas_call(
@@ -660,9 +676,9 @@
             pltpu.VMEM((mp_parts - 1, tokens, part), y.dtype),
             pltpu.VMEM(selected.shape, selected.dtype),
             pltpu.VMEM(selected.shape, selected.dtype),
-            pltpu.VMEM((reduce_sizes(piece, row_parts, mp_parts), BLOCK), selected.dtype),
-            pltpu.VMEM((2,) + chunk, kept.dtype),
-            pltpu.VMEM((2,) + chunk, kept.dtype),
+            pltpu.VMEM((reduce_sizes(selected.shape[0]), BLOCK), selected.dtype),
+            pltpu.VMEM((4,) + chunk, kept.dtype),
+            pltpu.VMEM((4,) + chunk, kept.dtype),
             pltpu.SemaphoreType.DMA((copies,)),
             pltpu.SemaphoreType.DMA((copies,)),
         ],

time: 251 us -> 240 us (0.956)
  Pallas kernels: 241 us -> 230 us
    pallas_call x1, Pallas kernels: 110 us -> 99.4 us  [solve(): pl.pallas_call(solve_kernel, out_shape=(jax.ShapeDtypeStruct((part, order...]
where the time goes in v3:
time: 240 us
  Pallas kernels  230 us (96%)
  local copies, waits for them, and re-layouts  5.73 us (2%)
  other arithmetic  3.54 us (1%)
    pallas_call x1, Pallas kernels, solve(): pl.pallas_call(solve_kernel, out_shape=(jax.ShapeDtypeStruct((part, order...  99.4 us
    pallas_call x1, Pallas kernels, gather(): pl.pallas_call(gather_kernel, out_shape=(jax.ShapeDtypeStruct(low.shape,...  57.9 us
    pallas_call x1, Pallas kernels, exchange(): pl.pallas_call(exchange_kernel, out_shape=(jax.ShapeDtypeStruct((mp_parts...  44.7 us
    pallas_call x1, Pallas kernels, pick_columns(): pl.pallas_call(pick_columns_kernel, out_shape=(jax.ShapeDtypeStruct((rows...  6.74 us
    pallas_call x1, Pallas kernels, prune(): pl.pallas_call(prune_kernel, out_shape=jax.ShapeDtypeStruct((rows, width)...  6.64 us
    unnamed x12, local copies, waits for them, and re-layouts  5.73 us
    pallas_call x1, Pallas kernels, pick_rows(): pl.pallas_call(pick_rows_kernel, out_shape=jax.ShapeDtypeStruct((blocks *...  5.27 us
    pallas_call x1, Pallas kernels, gram_of(): pl.pallas_call(functools.partial(gram_kernel, row_parts, mp_parts), grid=...  4.85 us

profile of v3, /device:TPU:0, one launch (start us, length us, event | category | flops | bytes accessed | tf_op | source)
XLA Modules:
  0.0 239.7 jit_solution(6151640155300743563)
XLA Ops:
  0.7 0.8 compare_reduce_fusion.1
  1.6 0.7 compare_reduce_fusion
  2.3 0.7 fusion
  3.0 0.7 fusion.3
  3.6 0.6 pad_add_fusion.places_ref
  4.2 5.3 %shard_map.62.kept_ref = bf16[896,2048]{1,0:T(8,128)(2,1)} custom-call(s32[4,7]{1,0:T(4,128)} %pad_add_fusion.places_ref, bf16[1024,2048]{1,0:T(8,128)(2,1)} %weight_ref.5), custom_call_target="tpu_custom_call" | custom-call | tf_op jit(solution)/shard_map/pallas_call | solution.py:450
  9.5 0.0 copy-start.4
  9.5 0.0 copy-start.5
  9.5 6.7 %shard_map.59 = (f32[1024,896]{1,0:T(8,128)}, f32[3584,128]{1,0:T(8,128)}) custom-call(s32[4,7]{1,0:T(4,128)} %pad_add_fusion.places_ref, f32[1024,2048]{1,0:T(8,128)} %factor_ref.1), custom_call_target="tpu_custom_call" | custom-call | tf_op jit(solution)/shard_map/pallas_call | solution.py:419
  16.2 0.0 copy-done.4
  16.3 1.5 copy-done.3
  17.8 57.9 %shard_map.60 = (f32[3584,128]{1,0:T(8,128)S(1)}, bf16[512,2048]{1,0:T(8,128)(2,1)S(1)}) custom-call(f32[3584,128]{1,0:T(8,128)S(1)} %copy-done.3, bf16[64,2048]{1,0:T(8,128)(2,1)S(1)} %copy-done.4), custom_call_target="tpu_custom_call" | custom-call | tf_op jit(solution)/shard_map/pallas_call | solution.py:344
  75.6 0.0 copy-done.5
  75.6 0.0 copy-start
  75.7 2.2 copy-done
  77.8 4.2 %shard_map.61 = (bf16[4,512,256]{2,1,0:T(8,128)(2,1)S(1)}, bf16[3584,128]{1,0:T(8,128)(2,1)S(1)}) custom-call(s32[4,7]{1,0:T(4,128)S(1)} %copy-done.5, bf16[512,2048]{1,0:T(8,128)(2,1)S(1)} %get-tuple-element.17.calib_ref, bf16[1024,2048]{1,0:T(8,128)(2,1)S(1)} %copy-done), custom_call_target="tpu_custom_call" | custom-call | tf_op jit(solution)/shard_map/pallas_call | solution.py:503
  82.0 0.0 copy-start.1
  82.1 99.4 %shard_map.63 = (bf16[256,896]{1,0:T(8,128)(2,1)S(1)}, bf16[512,256]{1,0:T(8,128)(2,1)S(1)}, bf16[896,2048]{1,0:T(8,128)(2,1)}) custom-call(f32[3584,128]{1,0:T(8,128)S(1)} %get-tuple-element.15.low_ref, f32[4,256,896]{2,1,0:T(8,128)} %bitcast.13, bf16[4,512,256]{2,1,0:T(8,128)(2,1)S(1)} %get-tuple-element.18.y_ref, ...), custom_call_target="tpu_custom_call" | custom-call | flops 60000002048 | bytes 6422528 | tf_op jit(solution)/shard_map/pallas_call | solution.py:656
  181.5 44.7 %shard_map.64 = (bf16[4,512,256]{2,1,0:T(8,128)(2,1)S(1)}, bf16[2,8,256,256]{3,2,1,0:T(8,128)(2,1)S(1)}, bf16[4,256,896]{2,1,0:T(8,128)(2,1)S(1)}) custom-call(bf16[512,256]{1,0:T(8,128)(2,1)S(1)} %get-tuple-element.20.out_ref, bf16[256,896]{1,0:T(8,128)(2,1)S(1)} %get-tuple-element.21.factor_ref), custom_call_target="tpu_custom_call" | custom-call | tf_op jit(solution)/shard_map/pallas_call | solution.py:759
  226.2 0.0 copy-done.1
  226.2 0.0 copy-start.2
  226.2 2.0 copy-done.2
  228.2 6.6 %shard_map.65 = bf16[1024,2048]{1,0:T(8,128)(2,1)} custom-call(s32[8]{0:T(128)S(1)} %convert_element_type.16.flags_ref, bf16[1024,2048]{1,0:T(8,128)(2,1)S(1)} %copy-done.1, bf16[1024,896]{1,0:T(8,128)(2,1)S(1)} %bitcast.11, bf16[896,2048]{1,0:T(8,128)(2,1)S(1)} %copy-done.2), custom_call_target="tpu_custom_call" | custom-call | tf_op jit(solution)/shard_map/pallas_call | solution.py:827
  234.9 4.9 %shard_map.66 = f32[1024,2048]{1,0:T(8,128)} custom-call(bf16[4,512,256]{2,1,0:T(8,128)(2,1)S(1)} %get-tuple-element.24.left_ref, bf16[2,8,256,256]{3,2,1,0:T(8,128)(2,1)S(1)} %get-tuple-element.25.right_ref), custom_call_target="tpu_custom_call" | custom-call | tf_op jit(solution)/shard_map/pallas_call | solution.py:799
  (5 shorter events, 0.0 us)
Async XLA Ops:
  9.5 6.7 %copy-start.4 = (bf16[64,2048]{1,0:T(8,128)(2,1)S(1)}, bf16[64,2048]{1,0:T(8,128)(2,1)}, u32[]{:S(2)}) copy-start(bf16[64,2048]{1,0:T(8,128)(2,1)} %calib_ref.1) | copy-start | bytes 786436
  9.5 66.1 %copy-start.5 = (s32[4,7]{1,0:T(4,128)S(1)}, s32[4,7]{1,0:T(4,128)}, u32[]{:S(2)}) copy-start(s32[4,7]{1,0:T(4,128)} %pad_add_fusion.places_ref) | copy-start | bytes 340
  16.3 1.5 copy-start.3
  75.6 2.2 copy-start
  82.0 144.2 %copy-start.1 = (bf16[1024,2048]{1,0:T(8,128)(2,1)S(1)}, bf16[1024,2048]{1,0:T(8,128)(2,1)}, u32[]{:S(2)}) copy-start(bf16[1024,2048]{1,0:T(8,128)(2,1)} %weight_ref.5) | copy-start | bytes 12582916
  226.2 2.0 copy-start.2

commit v4 on v3

--- a/solution.py
+++ b/solution.py
@@ -1,4 +1,5 @@
 import functools
+import math
 
 import jax
 import jax.numpy as jnp
@@ -11,6 +12,7 @@
 SUB = 8
 GROUP = 4
 TICKS = 4
+RING_GAP = 2
 MIB = 1024 * 1024
 VMEM = pl.BlockSpec(memory_space=pltpu.VMEM)
 SMEM = pl.BlockSpec(memory_space=pltpu.SMEM)
@@ -118,6 +120,21 @@
         )
 
 
+def room(*arrays):
+    total = 0
+    for shape, dtype in arrays:
+        width = jnp.dtype(dtype).itemsize
+        tile = SUB * 4 // width
+        lanes = -(-shape[-1] // BLOCK) * BLOCK
+        rows = -(-shape[-2] // tile) * tile
+        total += math.prod(shape[:-2]) * rows * lanes * width
+    return min(63 * MIB, total + total // 32 + MIB)
+
+
+def described(arrays):
+    return [(a.shape, a.dtype) for a in arrays]
+
+
 def greet(devices):
     barrier = pltpu.get_barrier_semaphore()
     for device in devices:
@@ -248,11 +265,12 @@
     return [functools.partial(step, s) for s in range(max(len(one) for one in lists))]
 
 
-def spread(steps, gap):
-    wide = []
-    for step in steps:
-        wide += [step] + [lambda: None] * (gap - 1)
-    return wide[: len(wide) - gap + 1]
+def placed(ticks, steps, start, gap):
+    for at, step in enumerate(steps):
+        if start + at * gap >= len(ticks):
+            return steps[at:]
+        ticks[start + at * gap].append(step)
+    return []
 
 
 def run_steps(*lists):
@@ -277,7 +295,7 @@
     return [{"rows": ring_member(place + 1)}, {"rows": ring_member(place - 1)}]
 
 
-def ring_sum_stages(links, src, recv, acc, out, sign, lanes):
+def ring_sum_stages(links, src, recv, out, sign, lanes):
     row_parts = lax.axis_size("rows")
     place = ring_place(lax.axis_index("rows"))
     to = {"rows": ring_member(place + sign)}
@@ -289,7 +307,7 @@
 
     stages = []
     for s in range(row_parts - 1):
-        source = src.at[chunk(0), lanes] if s == 0 else acc.at[s - 1]
+        source = src.at[chunk(0), lanes] if s == 0 else recv.at[s - 1]
         last = s == row_parts - 2
 
         def merge(s=s, last=last, rows=chunk(s + 1)):
@@ -297,7 +315,7 @@
             if last:
                 out[rows, lanes] = value
             else:
-                acc[s] = value
+                recv[s] = value
 
         stages.append(([links.copy(source, recv.at[s], to)], merge))
     for s in range(row_parts - 1):
@@ -320,45 +338,123 @@
 
 
 def gather_kernel(
-    src_ref, calib_ref, out_ref, all_calib_ref, acc_ref, recv_ref, send_sem, recv_sem
+    scale, places_ref, src_ref, calib_ref, weight_ref, out_ref, kept_ref, y_ref, sel_ref,
+    all_calib_ref, weight_vmem, chosen_ref, y_vmem, acc_ref, recv_ref, weight_sem, send_sem, recv_sem,
 ):
     row_parts = lax.axis_size("rows")
+    weight_copy = pltpu.make_async_copy(weight_ref, weight_vmem, weight_sem)
+    weight_copy.start()
     greet(everyone())
     links = Links(send_sem, recv_sem)
-    steps = joined(
-        reduce_lists(links, src_ref, acc_ref, recv_ref, out_ref),
+    steps = reduce_lists(links, src_ref, acc_ref, recv_ref, out_ref)
+    rings = joined(
         steps_of(ring_gather_stages(links, calib_ref, all_calib_ref, 1, row_parts // 2)),
         steps_of(ring_gather_stages(links, calib_ref, all_calib_ref, -1, row_parts // 2 - 1)),
     )
     steps[0]()
+    rings[0]()
     place = ring_place(lax.axis_index("rows"))
     size = calib_ref.shape[0]
     all_calib_ref[span(place * size, size, 16), :] = calib_ref[...]
-    for step in steps[1:]:
-        step()
-
-
-def gather(low, calib):
-    row_parts = lax.axis_size("rows")
+    weight_copy.wait()
+    for i in range(places_ref.shape[1]):
+        at = lax.broadcasted_iota(jnp.int32, (BLOCK, weight_vmem.shape[0]), 1)
+        row = lax.broadcasted_iota(jnp.int32, (BLOCK, weight_vmem.shape[0]), 0)
+        chosen = jnp.where(at == row + places_ref[4, i], 1.0, 0.0).astype(jnp.bfloat16)
+        chosen_ref[i * BLOCK : (i + 1) * BLOCK, :] = chosen
+
+    def pick(t, carry):
+        rows = pl.ds(pl.multiple_of(t * BLOCK, BLOCK), BLOCK)
+        value = jnp.dot(chosen_ref[rows, :], weight_vmem[...], preferred_element_type=jnp.float32)
+        kept_ref[rows, :] = value.astype(kept_ref.dtype)
+        return carry
+
+    count = places_ref.shape[1]
+    used = count * BLOCK
+    if kept_ref.shape[0] > used:
+        kept_ref[used:, :] = jnp.zeros((kept_ref.shape[0] - used, kept_ref.shape[1]), kept_ref.dtype)
+    steps[1]()
+    for at in range(max(len(steps) - 2, len(rings) - 1)):
+        if at + 2 < len(steps):
+            steps[at + 2]()
+        if at + 1 < len(rings):
+            rings[at + 1]()
+        low_at, high_at = at * count // 4, (at + 1) * count // 4
+        if high_at <= count:
+            lax.fori_loop(low_at, high_at, pick, 0)
+    project(scale, chosen_ref, all_calib_ref, weight_vmem, y_vmem, y_ref, sel_ref)
+
+
+def project(scale, chosen_ref, calib_ref, weight_ref, all_ref, y_ref, sel_ref):
+    mp_parts, tokens, part = y_ref.shape
+    tile = max(part, BLOCK)
+
+    def body(t, carry):
+        rows = pl.ds(pl.multiple_of(t * tile, tile), tile)
+        value = lax.dot_general(
+            calib_ref[...],
+            weight_ref[rows, :],
+            (((1,), (1,)), ((), ())),
+            preferred_element_type=jnp.float32,
+        )
+        value = (value * scale).astype(jnp.bfloat16)
+        all_ref[:, rows] = value
+        for s in range(tile // part):
+            y_ref[t * (tile // part) + s] = value[:, s * part : (s + 1) * part]
+        return carry
+
+    lax.fori_loop(0, weight_ref.shape[0] // tile, body, 0)
+    count = chosen_ref.shape[0] // BLOCK
+    for i in range(count):
+        value = lax.dot_general(
+            all_ref[...],
+            chosen_ref[i * BLOCK : (i + 1) * BLOCK, :],
+            (((1,), (1,)), ((), ())),
+            preferred_element_type=jnp.float32,
+        )
+        sel_ref[i * tokens : (i + 1) * tokens, :] = value.astype(sel_ref.dtype)
+    used = count * tokens
+    if sel_ref.shape[0] > used:
+        sel_ref[used:, :] = jnp.zeros((sel_ref.shape[0] - used, BLOCK), sel_ref.dtype)
+
+
+def gather(places, low, calib, weight, scale):
+    row_parts, mp_parts = lax.axis_size("rows"), lax.axis_size("mp")
+    tokens = calib.shape[0] * row_parts
     count = reduce_count() + row_parts - 1
+    unit = 16 * row_parts
+    kept = -(-places.shape[1] * BLOCK // unit) * unit
+    outs = (
+        jax.ShapeDtypeStruct(low.shape, low.dtype),
+        jax.ShapeDtypeStruct((kept, weight.shape[1]), weight.dtype),
+        jax.ShapeDtypeStruct((mp_parts, tokens, weight.shape[0] // mp_parts), weight.dtype),
+        jax.ShapeDtypeStruct((padded(places.shape[1] * tokens), BLOCK), weight.dtype),
+    )
+    scratch = [
+        ((tokens, calib.shape[1]), calib.dtype),
+        (weight.shape, weight.dtype),
+        ((places.shape[1] * BLOCK, weight.shape[0]), weight.dtype),
+        ((tokens, weight.shape[0]), weight.dtype),
+        (low.shape, low.dtype),
+        ((reduce_sizes(low.shape[0]), BLOCK), low.dtype),
+    ]
     return pl.pallas_call(
-        gather_kernel,
-        out_shape=(
-            jax.ShapeDtypeStruct(low.shape, low.dtype),
-            jax.ShapeDtypeStruct((calib.shape[0] * row_parts, calib.shape[1]), calib.dtype),
-        ),
-        in_specs=[VMEM, VMEM],
-        out_specs=(VMEM, VMEM),
-        scratch_shapes=[
-            pltpu.VMEM(low.shape, low.dtype),
-            pltpu.VMEM((reduce_sizes(low.shape[0]), BLOCK), low.dtype),
+        functools.partial(gather_kernel, scale),
+        out_shape=outs,
+        in_specs=[SMEM, VMEM, VMEM, pl.BlockSpec(memory_space=pltpu.HBM)],
+        out_specs=(VMEM, VMEM, VMEM, VMEM),
+        scratch_shapes=[pltpu.VMEM(*one) for one in scratch]
+        + [
+            pltpu.SemaphoreType.DMA,
             pltpu.SemaphoreType.DMA((count,)),
             pltpu.SemaphoreType.DMA((count,)),
         ],
         compiler_params=pltpu.CompilerParams(
-            collective_id=1, has_side_effects=True, vmem_limit_bytes=24 * MIB
+            collective_id=1,
+            has_side_effects=True,
+            vmem_limit_bytes=room(*described(outs), *described((low, calib)), *scratch),
         ),
-    )(low, calib)
+    )(places, low, calib, weight)
 
 
 def scatter_steps(links, src, acc, recv, out):
@@ -434,95 +530,7 @@
     )(places, factor)
 
 
-def pick_rows_kernel(places_ref, weight_ref, out_ref):
-    step = pl.program_id(0)
-    count = places_ref.shape[1]
-    inside = (places_ref[3, jnp.minimum(step, count - 1)] != 0) & (step < count)
-    value = weight_ref[...].astype(jnp.float32)
-    out_ref[...] = jnp.where(inside, value, 0.0).astype(jnp.bfloat16)
-
-
-def pick_rows(places, weight):
-    count = places.shape[1]
-    width = weight.shape[1]
-    unit = 16 * lax.axis_size("rows")
-    blocks = -(-(-(-count * BLOCK // unit) * unit) // BLOCK)
-    return pl.pallas_call(
-        pick_rows_kernel,
-        out_shape=jax.ShapeDtypeStruct((blocks * BLOCK, width), jnp.bfloat16),
-        grid_spec=pltpu.PrefetchScalarGridSpec(
-            num_scalar_prefetch=1,
-            grid=(blocks,),
-            in_specs=[
-                pl.BlockSpec(
-                    (BLOCK, width), lambda i, places: (places[2, jnp.minimum(i, count - 1)], 0)
-                )
-            ],
-            out_specs=pl.BlockSpec((BLOCK, width), lambda i, places: (i, 0)),
-        ),
-    )(places, weight)
-
-
-def project_kernel(scale, places_ref, calib_ref, weight_ref, y_ref, sel_ref):
-    step = pl.program_id(0)
-    count = places_ref.shape[1]
-    tokens = calib_ref.shape[0]
-    tile = weight_ref.shape[0]
-    part = y_ref.shape[2]
-
-    @pl.when(step == 0)
-    def _():
-        sel_ref[...] = jnp.zeros(sel_ref.shape, sel_ref.dtype)
-
-    value = lax.dot_general(
-        calib_ref[...],
-        weight_ref[...],
-        (((1,), (1,)), ((), ())),
-        preferred_element_type=jnp.float32,
-    )
-    value = (value * scale).astype(jnp.bfloat16)
-    for s in range(tile // part):
-        y_ref[s] = value[:, s * part : (s + 1) * part]
-    for i in range(count):
-        for s in range(tile // BLOCK):
-            here = step * (tile // BLOCK) + s
-
-            @pl.when((places_ref[3, i] != 0) & (places_ref[2, i] == here))
-            def _():
-                sel_ref[i * tokens : (i + 1) * tokens, :] = value[:, s * BLOCK : (s + 1) * BLOCK]
-
-
-def project(places, calib, weight, scale):
-    count = places.shape[1]
-    tokens, width = calib.shape
-    rows = weight.shape[0]
-    mp_parts = lax.axis_size("mp")
-    part = rows // mp_parts
-    tile = max(part, BLOCK)
-    sel_rows = padded(count * tokens)
-    return pl.pallas_call(
-        functools.partial(project_kernel, scale),
-        out_shape=(
-            jax.ShapeDtypeStruct((mp_parts, tokens, part), jnp.bfloat16),
-            jax.ShapeDtypeStruct((sel_rows, BLOCK), jnp.bfloat16),
-        ),
-        grid_spec=pltpu.PrefetchScalarGridSpec(
-            num_scalar_prefetch=1,
-            grid=(rows // tile,),
-            in_specs=[
-                pl.BlockSpec((tokens, width), lambda i, places: (0, 0)),
-                pl.BlockSpec((tile, width), lambda i, places: (i, 0)),
-            ],
-            out_specs=(
-                pl.BlockSpec((tile // part, tokens, part), lambda i, places: (i, 0, 0)),
-                pl.BlockSpec((sel_rows, BLOCK), lambda i, places: (0, 0)),
-            ),
-        ),
-        compiler_params=pltpu.CompilerParams(vmem_limit_bytes=32 * MIB),
-    )(places, calib, weight)
-
-
-def invert(low_ref, out_ref, neg_ref, rhs_ref, pivot_ref, steps):
+def invert(low_ref, out_ref, neg_ref, rhs_ref, pivot_ref, ticks):
     count = out_ref.shape[0] // BLOCK
     at = 0
     for i in range(count):
@@ -534,8 +542,9 @@
                 out_ref[j * BLOCK : (j + 1) * BLOCK, i * BLOCK : (i + 1) * BLOCK] = block.T
 
     def tick(k, at):
-        for s in range(at, min(TICKS * count, len(steps)), TICKS):
-            pl.when(TICKS * k + at == s)(steps[s])
+        for s in range(at, len(ticks), TICKS):
+            if ticks[s]:
+                pl.when(TICKS * k + at == s)(lambda s=s: [step() for step in ticks[s]] and None)
 
     def stage(k, carry):
         tick(k, 0)
@@ -577,11 +586,9 @@
         return carry
 
     lax.fori_loop(0, count, stage, 0)
-    for s in range(TICKS * count, len(steps)):
-        steps[s]()
-
-
-def outputs_from(square_ref, columns_ref, y_ref, sel_ref, keep_ref, total_ref, factor_ref, out_ref):
+
+
+def outputs_from(square_ref, columns_ref, y_ref, sel_ref, gone, total_ref, factor_ref, out_ref):
     count = square_ref.shape[0] // BLOCK
     tokens = y_ref.shape[0]
     total_ref[...] = jnp.zeros(total_ref.shape, jnp.float32)
@@ -605,90 +612,8 @@
     update = lax.dot_general(
         selected, factor_ref[...], (((1,), (1,)), ((), ())), preferred_element_type=jnp.float32
     )
-    value = jnp.where(keep_ref[...] != 0.0, y_ref[...] - update, 0.0)
+    value = jnp.where(gone == 0, y_ref[...] - update, 0.0)
     out_ref[...] = value.astype(jnp.bfloat16)
-
-
-def solve_kernel(
-    low_ref, columns_ref, y_ref, sel_ref, keep_ref, kept_ref,
-    factor_ref, out_ref, all_kept_ref,
-    square_ref, neg_ref, rhs_ref, pivot_ref, total_ref,
-    own_columns_ref, c_acc, c_recv, own_ref, y_acc, y_recv, all_ref, acc_ref, recv_ref,
-    k_acc, k_recv, send_sem, recv_sem,
-):
-    greet(everyone())
-    links = Links(send_sem, recv_sem)
-    sum_steps = joined(
-        reduce_lists(links, sel_ref, acc_ref, recv_ref, all_ref),
-        steps_of(scatter_steps(links, y_ref, y_acc, y_recv, own_ref)),
-    )
-    lanes = kept_ref.shape[1] // 4
-    rings = []
-    for at in range(4):
-        stages = ring_sum_stages(
-            links,
-            kept_ref,
-            k_recv.at[at],
-            k_acc.at[at],
-            all_kept_ref,
-            1 - 2 * (at % 2),
-            slice(at * lanes, (at + 1) * lanes),
-        )
-        rings.append([lambda: None] * (at // 2) + spread(steps_of(stages), 2))
-    steps = joined(
-        *rings,
-        spread(sum_steps, TICKS),
-        spread(steps_of(scatter_steps(links, columns_ref, c_acc, c_recv, own_columns_ref)), 3 * TICKS),
-    )
-    invert(low_ref, square_ref, neg_ref, rhs_ref, pivot_ref, steps)
-    outputs_from(
-        square_ref, own_columns_ref, own_ref, all_ref, keep_ref, total_ref, factor_ref, out_ref
-    )
-
-
-def solve(low, columns, y, selected, keep, kept):
-    row_parts, mp_parts = lax.axis_size("rows"), lax.axis_size("mp")
-    copies = reduce_count() + 2 * bits_of(mp_parts)
-    copies += 8 * (row_parts - 1)
-    chunk = (row_parts - 1, kept.shape[0] // row_parts, kept.shape[1] // 4)
-    _, part, order = columns.shape
-    tokens = y.shape[1]
-    return pl.pallas_call(
-        solve_kernel,
-        out_shape=(
-            jax.ShapeDtypeStruct((part, order), jnp.bfloat16),
-            jax.ShapeDtypeStruct((tokens, part), jnp.bfloat16),
-            jax.ShapeDtypeStruct(kept.shape, kept.dtype),
-        ),
-        in_specs=[VMEM] * 6,
-        out_specs=(VMEM, VMEM, VMEM),
-        scratch_shapes=[
-            pltpu.VMEM((order, order), jnp.float32),
-            pltpu.VMEM((BLOCK, BLOCK), jnp.float32),
-            pltpu.VMEM((6 * BLOCK, order), jnp.bfloat16),
-            pltpu.VMEM((BLOCK, order), jnp.float32),
-            pltpu.VMEM((part, order), jnp.float32),
-            pltpu.VMEM((part, order), jnp.float32),
-            pltpu.VMEM(columns.shape, jnp.float32),
-            pltpu.VMEM((mp_parts - 1, part, order), jnp.float32),
-            pltpu.VMEM((tokens, part), jnp.float32),
-            pltpu.VMEM(y.shape, y.dtype),
-            pltpu.VMEM((mp_parts - 1, tokens, part), y.dtype),
-            pltpu.VMEM(selected.shape, selected.dtype),
-            pltpu.VMEM(selected.shape, selected.dtype),
-            pltpu.VMEM((reduce_sizes(selected.shape[0]), BLOCK), selected.dtype),
-            pltpu.VMEM((4,) + chunk, kept.dtype),
-            pltpu.VMEM((4,) + chunk, kept.dtype),
-            pltpu.SemaphoreType.DMA((copies,)),
-            pltpu.SemaphoreType.DMA((copies,)),
-        ],
-        compiler_params=pltpu.CompilerParams(
-            collective_id=2, has_side_effects=True, vmem_limit_bytes=48 * MIB
-        ),
-        cost_estimate=pl.CostEstimate(
-            flops=60_000_000_000, bytes_accessed=2 * order * order * 4, transcendentals=0
-        ),
-    )(low, columns, y, selected, keep, kept)
 
 
 def moved_to(r, m, row_parts, mp_parts):
@@ -703,30 +628,17 @@
     return first, second
 
 
-def exchange_kernel(out_ref, factor_ref, left_ref, right_ref, all_factor_ref, send_sem, recv_sem):
+def exchange_lists(links, out_ref, factor_ref, left_ref, right_ref, all_factor_ref):
     row_parts, mp_parts = lax.axis_size("rows"), lax.axis_size("mp")
     r, m = lax.axis_index("rows"), lax.axis_index("mp")
-    per = row_parts // mp_parts
     tokens = out_ref.shape[0]
     to_row, to_mp = moved_to(r, m, row_parts, mp_parts)
-    from_row = m * per + r % per
-    from_mp = lax.rem(r // per + mp_parts - 1, mp_parts)
-    devices = [{"mp": flip(m, k)} for k in range(bits_of(mp_parts))]
-    devices += [{"rows": flip(r, k)} for k in range(bits_of(row_parts))]
     target = {"rows": to_row, "mp": to_mp}
-    devices += [target, {"rows": from_row, "mp": from_mp}]
-    greet(devices)
-    links = Links(send_sem, recv_sem)
-    mine = reversed_bits(m, mp_parts)
-
-    orders = right_orders(row_parts)
     lists = []
-    for h, order in enumerate(orders):
+    for h, order in enumerate(right_orders(row_parts)):
         half = tokens // 2
         slot = ordered_bits(to_row, order)
-        copy = links.copy(
-            out_ref.at[pl.ds(h * half, half)], right_ref.at[h, slot], target
-        )
+        copy = links.copy(out_ref.at[pl.ds(h * half, half)], right_ref.at[h, slot], target)
         stages = [([copy], None)]
         base, size = ordered_bits(r, order), 1
         for k in reversed(order):
@@ -737,7 +649,7 @@
         lists.append(steps_of(stages))
     for src, dst in ((out_ref, left_ref), (factor_ref, all_factor_ref)):
         stages = []
-        base, size = mine, 1
+        base, size = reversed_bits(m, mp_parts), 1
         for k in reversed(range(bits_of(mp_parts))):
             region = dst.at[pl.ds(base, size)]
             source = src if size == 1 else region
@@ -746,33 +658,113 @@
             base = base - ((base // size) % 2) * size
             size *= 2
         lists.append(steps_of(stages))
+    return lists
+
+
+def solve_kernel(
+    blocks_ref, low_ref, columns_ref, y_ref, sel_ref, kept_ref,
+    left_ref, right_ref, all_factor_ref, all_kept_ref,
+    factor_ref, out_ref, square_ref, neg_ref, rhs_ref, pivot_ref, total_ref,
+    own_columns_ref, c_acc, c_recv, own_ref, y_acc, y_recv, all_ref, acc_ref, recv_ref,
+    k_recv, send_sem, recv_sem,
+):
+    row_parts, mp_parts = lax.axis_size("rows"), lax.axis_size("mp")
+    r, m = lax.axis_index("rows"), lax.axis_index("mp")
+    to_row, to_mp = moved_to(r, m, row_parts, mp_parts)
+    from_row = m * (row_parts // mp_parts) + r % (row_parts // mp_parts)
+    from_mp = lax.rem(r // (row_parts // mp_parts) + mp_parts - 1, mp_parts)
+    greet(everyone() + [{"rows": to_row, "mp": to_mp}, {"rows": from_row, "mp": from_mp}])
+    links = Links(send_sem, recv_sem)
+    ticks = [[] for _ in range(TICKS * (square_ref.shape[0] // BLOCK))]
+    sum_steps = joined(
+        reduce_lists(links, sel_ref, acc_ref, recv_ref, all_ref),
+        steps_of(scatter_steps(links, y_ref, y_acc, y_recv, own_ref)),
+    )
+    column_steps = steps_of(scatter_steps(links, columns_ref, c_acc, c_recv, own_columns_ref))
+    late = placed(ticks, sum_steps, 0, TICKS) + placed(ticks, column_steps, 0, 3 * TICKS)
+    lanes = kept_ref.shape[1] // 4
+    rings = []
+    for at in range(4):
+        stages = ring_sum_stages(
+            links,
+            kept_ref,
+            k_recv.at[at],
+            all_kept_ref,
+            1 - 2 * (at % 2),
+            slice(at * lanes, (at + 1) * lanes),
+        )
+        rings.append(placed(ticks, steps_of(stages), RING_GAP // 2 * (at // 2), RING_GAP))
+    invert(low_ref, square_ref, neg_ref, rhs_ref, pivot_ref, ticks)
+    for step in late:
+        step()
+    part = own_ref.shape[1]
+    start = (r * mp_parts + reversed_bits(m, mp_parts)) * part
+    feature = start + lax.broadcasted_iota(jnp.int32, (1, part), 1)
+    gone = jnp.zeros((1, part), jnp.int32)
+    for i in range(blocks_ref.shape[0]):
+        first = blocks_ref[i] * BLOCK
+        gone = jnp.where((feature >= first) & (feature < first + BLOCK), 1, gone)
+    outputs_from(
+        square_ref, own_columns_ref, own_ref, all_ref, gone, total_ref, factor_ref, out_ref
+    )
+    lists = exchange_lists(links, out_ref, factor_ref, left_ref, right_ref, all_factor_ref)
+    steps = joined(*lists, *rings)
+    steps[0]()
+    mine = reversed_bits(m, mp_parts)
     left_ref[mine] = out_ref[...]
     all_factor_ref[mine] = factor_ref[...]
-    run_steps(*lists)
-
-
-def exchange(outputs, factor):
+    for step in steps[1:]:
+        step()
+
+
+def solve(blocks, low, columns, y, selected, kept):
     row_parts, mp_parts = lax.axis_size("rows"), lax.axis_size("mp")
-    tokens, part = outputs.shape
-    order = factor.shape[1]
-    count = 2 * (1 + bits_of(row_parts)) + 2 * bits_of(mp_parts)
+    copies = reduce_count() + 4 * bits_of(mp_parts) + 8 * (row_parts - 1)
+    copies += 2 * (1 + bits_of(row_parts))
+    chunk = (row_parts - 1, kept.shape[0] // row_parts, kept.shape[1] // 4)
+    _, part, order = columns.shape
+    tokens = y.shape[1]
+    outs = (
+        jax.ShapeDtypeStruct((mp_parts, tokens, part), jnp.bfloat16),
+        jax.ShapeDtypeStruct((2, row_parts, tokens // 2, part), jnp.bfloat16),
+        jax.ShapeDtypeStruct((mp_parts, part, order), jnp.bfloat16),
+        jax.ShapeDtypeStruct(kept.shape, kept.dtype),
+    )
+    scratch = [
+        ((part, order), jnp.bfloat16),
+        ((tokens, part), jnp.bfloat16),
+        ((order, order), jnp.float32),
+        ((BLOCK, BLOCK), jnp.float32),
+        ((6 * BLOCK, order), jnp.bfloat16),
+        ((BLOCK, order), jnp.float32),
+        ((part, order), jnp.float32),
+        ((part, order), jnp.float32),
+        (columns.shape, jnp.float32),
+        ((mp_parts - 1, part, order), jnp.float32),
+        ((tokens, part), jnp.float32),
+        (y.shape, y.dtype),
+        ((mp_parts - 1, tokens, part), y.dtype),
+        (selected.shape, selected.dtype),
+        (selected.shape, selected.dtype),
+        ((reduce_sizes(selected.shape[0]), BLOCK), selected.dtype),
+        ((4,) + chunk, kept.dtype),
+    ]
     return pl.pallas_call(
-        exchange_kernel,
-        out_shape=(
-            jax.ShapeDtypeStruct((mp_parts, tokens, part), jnp.bfloat16),
-            jax.ShapeDtypeStruct((2, row_parts, tokens // 2, part), jnp.bfloat16),
-            jax.ShapeDtypeStruct((mp_parts, part, order), jnp.bfloat16),
+        solve_kernel,
+        out_shape=outs,
+        in_specs=[SMEM] + [VMEM] * 5,
+        out_specs=(VMEM, VMEM, VMEM, VMEM),
+        scratch_shapes=[pltpu.VMEM(*one) for one in scratch]
+        + [pltpu.SemaphoreType.DMA((copies,)), pltpu.SemaphoreType.DMA((copies,))],
+        compiler_params=pltpu.CompilerParams(
+            collective_id=2,
+            has_side_effects=True,
+            vmem_limit_bytes=room(*described(outs), *described((low, columns, y, selected, kept)), *scratch),
         ),
-        in_specs=[VMEM, VMEM],
-        out_specs=(VMEM, VMEM, VMEM),
-        scratch_shapes=[
-            pltpu.SemaphoreType.DMA((count,)),
-            pltpu.SemaphoreType.DMA((count,)),
-        ],
-        compiler_params=pltpu.CompilerParams(
-            collective_id=3, has_side_effects=True, vmem_limit_bytes=32 * MIB
+        cost_estimate=pl.CostEstimate(
+            flops=60_000_000_000, bytes_accessed=2 * order * order * 4, transcendentals=0
         ),
-    )(outputs, factor)
+    )(blocks, low, columns, y, selected, kept)
 
 
 def gram_kernel(row_parts, mp_parts, left_ref, right_ref, out_ref):
@@ -806,21 +798,25 @@
     )(left, right)
 
 
-def prune_kernel(flags_ref, weight_ref, factor_ref, kept_ref, out_ref):
+def prune_kernel(blocks_ref, weight_ref, factor_ref, kept_ref, out_ref):
     step = pl.program_id(0)
     tile, width = weight_ref.shape
+    row_block = lax.axis_index("rows") * pl.num_programs(0) * (tile // BLOCK)
     chunk = min(width, 512)
     for c in range(width // chunk):
         lanes = slice(c * chunk, (c + 1) * chunk)
         update = jnp.dot(factor_ref[...], kept_ref[:, lanes], preferred_element_type=jnp.float32)
         value = weight_ref[:, lanes].astype(jnp.float32) - update
         for s in range(tile // BLOCK):
-            gone = flags_ref[step * (tile // BLOCK) + s] != 0
+            here = row_block + step * (tile // BLOCK) + s
+            gone = blocks_ref[0] == here
+            for i in range(1, blocks_ref.shape[0]):
+                gone = gone | (blocks_ref[i] == here)
             rows = slice(s * BLOCK, (s + 1) * BLOCK)
             out_ref[rows, lanes] = jnp.where(gone, 0.0, value[rows, :]).astype(jnp.bfloat16)
 
 
-def prune(flags, weight, factor, kept_rows):
+def prune(blocks, weight, factor, kept_rows):
     rows, width = weight.shape
     order = factor.shape[1]
     tile = min(rows, 256)
@@ -831,14 +827,14 @@
             num_scalar_prefetch=1,
             grid=(rows // tile,),
             in_specs=[
-                pl.BlockSpec((tile, width), lambda i, flags: (i, 0)),
-                pl.BlockSpec((tile, order), lambda i, flags: (i, 0)),
-                pl.BlockSpec((order, width), lambda i, flags: (0, 0)),
+                pl.BlockSpec((tile, width), lambda i, blocks: (i, 0)),
+                pl.BlockSpec((tile, order), lambda i, blocks: (i, 0)),
+                pl.BlockSpec((order, width), lambda i, blocks: (0, 0)),
             ],
-            out_specs=pl.BlockSpec((tile, width), lambda i, flags: (i, 0)),
+            out_specs=pl.BlockSpec((tile, width), lambda i, blocks: (i, 0)),
         ),
         compiler_params=pltpu.CompilerParams(vmem_limit_bytes=32 * MIB),
-    )(flags, weight, factor, kept_rows)
+    )(blocks, weight, factor, kept_rows)
 
 
 def shards(calib, weight, inverse_factor, pruned_blocks):
@@ -858,24 +854,20 @@
             ((col_offsets >= 0) & (col_offsets < width_dev)).astype(jnp.int32),
             jnp.clip(row_offsets, 0, rows_dev - BLOCK) // BLOCK,
             ((row_offsets >= 0) & (row_offsets < rows_dev)).astype(jnp.int32),
+            row_offsets,
         ]
     ).astype(jnp.int32)
-    block_ids = row_start // BLOCK + jnp.arange(rows_dev // BLOCK, dtype=jnp.int32)
-    flags = jnp.any(block_ids[:, None] == pruned_blocks[None, :], axis=1).astype(jnp.int32)
-    own_start = row_start + reversed_bits(m, mp_parts) * part
-    own_ids = (own_start + jnp.arange(part, dtype=jnp.int32)) // BLOCK
-    keep = 1.0 - jnp.any(own_ids[:, None] == pruned_blocks[None, :], axis=1).astype(jnp.float32)
-
-    own_kept = pick_rows(places, weight)
     columns, own_low = pick_columns(places, inverse_factor)
     columns = columns.reshape(mp_parts, part, columns.shape[1])
-    low, all_calib = gather(own_low, calib)
-    y, own_selected = project(places, all_calib, weight, float(full_width) ** (-0.5))
-    factor, outputs, kept_rows = solve(low, columns, y, own_selected, keep[None, :], own_kept)
-    left, right, all_factor = exchange(outputs, factor)
+    low, own_kept, y, own_selected = gather(
+        places, own_low, calib, weight, float(full_width) ** (-0.5)
+    )
+    left, right, all_factor, kept_rows = solve(
+        pruned_blocks, low, columns, y, own_selected, own_kept
+    )
     gram_block = gram_of(left, right)
     pruned_weight = prune(
-        flags, weight, all_factor.reshape(rows_dev, factor.shape[1]), kept_rows
+        pruned_blocks, weight, all_factor.reshape(rows_dev, all_factor.shape[2]), kept_rows
     )
     return (pruned_weight, gram_block)
 

time: 240 us -> 228 us (0.950)
  Pallas kernels: 230 us -> 218 us
  local copies, waits for them, and re-layouts: 5.73 us -> 8.16 us
    pallas_call x5 -> x2, Pallas kernels: 211 us -> 199 us  [the longest x1 141 us: solve(): pl.pallas_call(solve_kernel, out_shape=outs, in_specs=[SMEM] + [VMEM] * 5...]
    unnamed x12 -> x16, local copies, waits for them, and re-layouts: 5.73 us -> 7.56 us
where the time goes in v4:
time: 228 us
  Pallas kernels  218 us (96%)
  local copies, waits for them, and re-layouts  8.16 us (4%)
    pallas_call x1, Pallas kernels, solve(): pl.pallas_call(solve_kernel, out_shape=outs, in_specs=[SMEM] + [VMEM] * 5...  141 us
    pallas_call x1, Pallas kernels, gather(): pl.pallas_call(functools.partial(gather_kernel, scale), out_shape=outs, i...  57.8 us
    pallas_call x1, Pallas kernels, pick_columns(): pl.pallas_call(pick_columns_kernel, out_shape=(jax.ShapeDtypeStruct((rows...  7.91 us
    unnamed x16, local copies, waits for them, and re-layouts  7.56 us
    pallas_call x1, Pallas kernels, prune(): pl.pallas_call(prune_kernel, out_shape=jax.ShapeDtypeStruct((rows, width)...  6.62 us
    pallas_call x1, Pallas kernels, gram_of(): pl.pallas_call(functools.partial(gram_kernel, row_parts, mp_parts), grid=...  4.85 us

profile of v4, /device:TPU:0, one launch (start us, length us, event | category | flops | bytes accessed | tf_op | source)
XLA Modules:
  0.0 228.2 jit_solution(6763961038233101698)
XLA Ops:
  0.6 0.7 fusion.1
  1.3 0.7 fusion.4
  2.0 0.6 stack.31.places_ref
  2.6 0.0 copy-start.4
  2.6 0.0 copy-start.5
  2.6 7.9 %shard_map.59 = (f32[1024,896]{1,0:T(8,128)}, f32[3584,128]{1,0:T(8,128)}) custom-call(s32[5,7]{1,0:T(8,128)} %stack.31.places_ref, f32[1024,2048]{1,0:T(8,128)} %factor_ref.1), custom_call_target="tpu_custom_call" | custom-call | tf_op jit(solution)/shard_map/pallas_call | solution.py:515
  10.5 0.0 copy-start.6
  10.5 0.0 copy-done.4
  10.5 0.0 copy-done.5
  10.5 0.0 copy-start
  10.5 2.2 copy-done
  12.7 0.0 copy-start.3
  12.7 1.5 copy-done.3
  14.2 57.8 %shard_map.60 = (f32[3584,128]{1,0:T(8,128)S(1)}, bf16[896,2048]{1,0:T(8,128)(2,1)S(1)}, bf16[4,512,256]{2,1,0:T(8,128)(2,1)S(1)}, bf16[3584,128]{1,0:T(8,128)(2,1)S(1)}) custom-call(s32[5,7]{1,0:T(8,128)S(1)} %copy-done.5, f32[3584,128]{1,0:T(8,128)S(1)} %copy-done.3, bf16[64,2048]{1,0:T(8,128)(2,1)S(1)} %copy-done.4, bf16[1024,2048]{1,0:T(8,128)(2,1)S(1)} %copy-done), custom_call_target="tpu_custom_call" | custom-call | tf_op jit(solution)/shard_map/pallas_call | solution.py:441
  72.0 0.0 copy-start.7
  72.1 1.8 copy-done.7
  73.9 0.0 copy-done.6
  73.9 0.0 copy-start.1
  73.9 140.8 %shard_map.61 = (bf16[4,512,256]{2,1,0:T(8,128)(2,1)S(1)}, bf16[2,8,256,256]{3,2,1,0:T(8,128)(2,1)S(1)}, bf16[4,256,896]{2,1,0:T(8,128)(2,1)S(1)}, bf16[896,2048]{1,0:T(8,128)(2,1)}) custom-call(s32[7]{0:T(128)S(1)} %copy-done.6, f32[3584,128]{1,0:T(8,128)S(1)} %get-tuple-element.13.low_ref, f32[4,256,896]{2,1,0:T(8,128)} %bitcast.13, ...), custom_call_target="tpu_custom_call" | custom-call | flops 60000002048 | bytes 6422528 | tf_op jit(solution)/shard_map/pallas_call | solution.py:752
  214.7 0.0 copy-done.1
  214.7 0.0 copy-start.2
  214.7 2.0 copy-done.2
  216.8 6.6 %shard_map.62 = bf16[1024,2048]{1,0:T(8,128)(2,1)} custom-call(s32[7]{0:T(128)S(1)} %copy-done.6, bf16[1024,2048]{1,0:T(8,128)(2,1)S(1)} %copy-done.1, bf16[1024,896]{1,0:T(8,128)(2,1)S(1)} %bitcast.12, bf16[896,2048]{1,0:T(8,128)(2,1)S(1)} %copy-done.2), custom_call_target="tpu_custom_call" | custom-call | tf_op jit(solution)/shard_map/pallas_call | solution.py:823
  223.4 4.9 %shard_map.63 = f32[1024,2048]{1,0:T(8,128)} custom-call(bf16[4,512,256]{2,1,0:T(8,128)(2,1)S(1)} %get-tuple-element.20.left_ref, bf16[2,8,256,256]{3,2,1,0:T(8,128)(2,1)S(1)} %get-tuple-element.21.right_ref), custom_call_target="tpu_custom_call" | custom-call | tf_op jit(solution)/shard_map/pallas_call | solution.py:791
Async XLA Ops:
  2.6 7.9 %copy-start.4 = (bf16[64,2048]{1,0:T(8,128)(2,1)S(1)}, bf16[64,2048]{1,0:T(8,128)(2,1)}, u32[]{:S(2)}) copy-start(bf16[64,2048]{1,0:T(8,128)(2,1)} %calib_ref.1) | copy-start | bytes 786436
  2.6 7.9 %copy-start.5 = (s32[5,7]{1,0:T(8,128)S(1)}, s32[5,7]{1,0:T(8,128)}, u32[]{:S(2)}) copy-start(s32[5,7]{1,0:T(8,128)} %stack.31.places_ref) | copy-start | bytes 424
  10.5 63.4 %copy-start.6 = (s32[7]{0:T(128)S(1)}, s32[7]{0:T(128)}, u32[]{:S(2)}) copy-start(s32[7]{0:T(128)} %blocks_ref.3) | copy-start | bytes 88
  10.5 2.2 copy-start
  12.7 1.5 copy-start.3
  72.0 1.8 copy-start.7
  73.9 140.8 %copy-start.1 = (bf16[1024,2048]{1,0:T(8,128)(2,1)S(1)}, bf16[1024,2048]{1,0:T(8,128)(2,1)}, u32[]{:S(2)}) copy-start(bf16[1024,2048]{1,0:T(8,128)(2,1)} %weight_ref.3) | copy-start | bytes 12582916
  214.7 2.0 copy-start.2

commit v5 on v4

--- a/solution.py
+++ b/solution.py
@@ -131,6 +131,11 @@
     return min(63 * MIB, total + total // 32 + MIB)
 
 
+def solve_room(passed, held):
+    whole = room(*passed, *held)
+    return whole if whole > 56 * MIB else room(*held)
+
+
 def described(arrays):
     return [(a.shape, a.dtype) for a in arrays]
 
@@ -152,11 +157,11 @@
     return devices
 
 
-def reduce_plans(rows):
+def reduce_plans(rows, split):
     pieces = lax.axis_size("rows") * lax.axis_size("mp")
     depth = bits_of(lax.axis_size("mp"))
     units = rows // (16 * pieces)
-    first = max(1, min(units - 1, (2 * units + 1) // 3))
+    first = max(1, min(units - 1, (2 * units + 1) // 3)) if split else units
     order = [f"mp{k}" for k in range(depth)]
     plans = [(0, 16 * first, order + ["rows"])]
     if units > first:
@@ -164,10 +169,10 @@
     return plans
 
 
-def reduce_sizes(rows):
+def reduce_sizes(rows, split):
     row_parts, mp_parts = lax.axis_size("rows"), lax.axis_size("mp")
     total = 0
-    for _, piece, order in reduce_plans(rows):
+    for _, piece, order in reduce_plans(rows, split):
         size = piece * row_parts * mp_parts
         for dim in order:
             parts = row_parts if dim == "rows" else 2
@@ -180,9 +185,9 @@
     return 4 * (bits_of(lax.axis_size("mp")) + lax.axis_size("rows") - 1)
 
 
-def reduce_lists(links, src, acc, recv, out):
+def reduce_lists(links, src, acc, recv, out, split):
     lists, off = [], 0
-    for start, piece, order in reduce_plans(src.shape[0]):
+    for start, piece, order in reduce_plans(src.shape[0], split):
         stages, off = reduce_stages(links, src, acc, recv, out, start, piece, order, off)
         lists.append(steps_of(stages))
     return joined(*lists)
@@ -346,7 +351,7 @@
     weight_copy.start()
     greet(everyone())
     links = Links(send_sem, recv_sem)
-    steps = reduce_lists(links, src_ref, acc_ref, recv_ref, out_ref)
+    steps = reduce_lists(links, src_ref, acc_ref, recv_ref, out_ref, True)
     rings = joined(
         steps_of(ring_gather_stages(links, calib_ref, all_calib_ref, 1, row_parts // 2)),
         steps_of(ring_gather_stages(links, calib_ref, all_calib_ref, -1, row_parts // 2 - 1)),
@@ -436,7 +441,7 @@
         ((places.shape[1] * BLOCK, weight.shape[0]), weight.dtype),
         ((tokens, weight.shape[0]), weight.dtype),
         (low.shape, low.dtype),
-        ((reduce_sizes(low.shape[0]), BLOCK), low.dtype),
+        ((reduce_sizes(low.shape[0], True), BLOCK), low.dtype),
     ]
     return pl.pallas_call(
         functools.partial(gather_kernel, scale),
@@ -677,7 +682,7 @@
     links = Links(send_sem, recv_sem)
     ticks = [[] for _ in range(TICKS * (square_ref.shape[0] // BLOCK))]
     sum_steps = joined(
-        reduce_lists(links, sel_ref, acc_ref, recv_ref, all_ref),
+        reduce_lists(links, sel_ref, acc_ref, recv_ref, all_ref, False),
         steps_of(scatter_steps(links, y_ref, y_acc, y_recv, own_ref)),
     )
     column_steps = steps_of(scatter_steps(links, columns_ref, c_acc, c_recv, own_columns_ref))
@@ -746,7 +751,7 @@
         ((mp_parts - 1, tokens, part), y.dtype),
         (selected.shape, selected.dtype),
         (selected.shape, selected.dtype),
-        ((reduce_sizes(selected.shape[0]), BLOCK), selected.dtype),
+        ((reduce_sizes(selected.shape[0], False), BLOCK), selected.dtype),
         ((4,) + chunk, kept.dtype),
     ]
     return pl.pallas_call(
@@ -759,7 +764,9 @@
         compiler_params=pltpu.CompilerParams(
             collective_id=2,
             has_side_effects=True,
-            vmem_limit_bytes=room(*described(outs), *described((low, columns, y, selected, kept)), *scratch),
+            vmem_limit_bytes=solve_room(
+                described(outs) + described((low, columns, y, selected)), described((kept,)) + scratch
+            ),
         ),
         cost_estimate=pl.CostEstimate(
             flops=60_000_000_000, bytes_accessed=2 * order * order * 4, transcendentals=0

time: 228 us -> 217 us (0.952)
  Pallas kernels: 218 us -> 210 us
  local copies, waits for them, and re-layouts: 8.16 us -> 4.3 us
    pallas_call x1, Pallas kernels: 141 us -> 132 us  [solve(): pl.pallas_call(solve_kernel, out_shape=outs, in_specs=[SMEM] + [VMEM] * 5...]
    unnamed x16 -> x14, local copies, waits for them, and re-layouts: 7.56 us -> 3.7 us
where the time goes in v5:
time: 217 us
  Pallas kernels  210 us (97%)
  local copies, waits for them, and re-layouts  4.3 us (2%)
    pallas_call x1, Pallas kernels, solve(): pl.pallas_call(solve_kernel, out_shape=outs, in_specs=[SMEM] + [VMEM] * 5...  132 us
    pallas_call x1, Pallas kernels, gather(): pl.pallas_call(functools.partial(gather_kernel, scale), out_shape=outs, i...  60.1 us
    pallas_call x1, Pallas kernels, pick_columns(): pl.pallas_call(pick_columns_kernel, out_shape=(jax.ShapeDtypeStruct((rows...  6.91 us
    pallas_call x1, Pallas kernels, prune(): pl.pallas_call(prune_kernel, out_shape=jax.ShapeDtypeStruct((rows, width)...  6.62 us
    pallas_call x1, Pallas kernels, gram_of(): pl.pallas_call(functools.partial(gram_kernel, row_parts, mp_parts), grid=...  4.85 us

profile of v5, /device:TPU:0, one launch (start us, length us, event | category | flops | bytes accessed | tf_op | source)
XLA Modules:
  0.0 216.6 jit_solution(7256874565664913728)
XLA Ops:
  0.6 0.7 fusion.1
  1.3 0.7 fusion.4
  2.0 0.6 stack.31.places_ref
  2.6 0.0 copy-start.3
  2.6 0.0 copy-start.4
  2.6 6.9 %shard_map.59 = (f32[1024,896]{1,0:T(8,128)}, f32[3584,128]{1,0:T(8,128)}) custom-call(s32[5,7]{1,0:T(8,128)} %stack.31.places_ref, f32[1024,2048]{1,0:T(8,128)} %factor_ref.1), custom_call_target="tpu_custom_call" | custom-call | tf_op jit(solution)/shard_map/pallas_call | solution.py:520
  9.5 0.0 copy-start.5
  9.5 0.0 copy-done.3
  9.5 0.0 copy-done.4
  9.5 0.0 copy-start
  9.5 2.2 %copy-done = bf16[1024,2048]{1,0:T(8,128)(2,1)S(1)} copy-done((bf16[1024,2048]{1,0:T(8,128)(2,1)S(1)}, bf16[1024,2048]{1,0:T(8,128)(2,1)}, u32[]{:S(2)}) %copy-start) | copy-done | bytes 4194328
  11.7 0.0 copy-start.2
  11.7 1.5 copy-done.2
  13.2 0.0 copy-start.6
  13.2 60.1 %shard_map.60 = (f32[3584,128]{1,0:T(8,128)S(1)}, bf16[896,2048]{1,0:T(8,128)(2,1)S(1)}, bf16[4,512,256]{2,1,0:T(8,128)(2,1)S(1)}, bf16[3584,128]{1,0:T(8,128)(2,1)S(1)}) custom-call(s32[5,7]{1,0:T(8,128)S(1)} %copy-done.4, f32[3584,128]{1,0:T(8,128)S(1)} %copy-done.2, bf16[64,2048]{1,0:T(8,128)(2,1)S(1)} %copy-done.3, bf16[1024,2048]{1,0:T(8,128)(2,1)S(1)} %copy-done), custom_call_target="tpu_custom_call" | custom-call | tf_op jit(solution)/shard_map/pallas_call | solution.py:446
  73.3 0.0 copy-done.5
  73.3 0.0 copy-done.6
  73.3 0.0 copy-start.1
  73.3 131.7 %shard_map.61 = (bf16[4,512,256]{2,1,0:T(8,128)(2,1)S(1)}, bf16[2,8,256,256]{3,2,1,0:T(8,128)(2,1)S(1)}, bf16[4,256,896]{2,1,0:T(8,128)(2,1)S(1)}, bf16[896,2048]{1,0:T(8,128)(2,1)S(1)}) custom-call(s32[7]{0:T(128)S(1)} %copy-done.5, f32[3584,128]{1,0:T(8,128)S(1)} %get-tuple-element.13.low_ref, f32[4,256,896]{2,1,0:T(8,128)S(1)} %bitcast.13, ...), custom_call_target="tpu_custom_call" | custom-call | flops 60000002048 | bytes 6422528 | tf_op jit(solution)/shard_map/pallas_call | solution.py:757
  205.1 0.0 copy-done.1
  205.1 6.6 %shard_map.62 = bf16[1024,2048]{1,0:T(8,128)(2,1)} custom-call(s32[7]{0:T(128)S(1)} %copy-done.5, bf16[1024,2048]{1,0:T(8,128)(2,1)S(1)} %copy-done.1, bf16[1024,896]{1,0:T(8,128)(2,1)S(1)} %bitcast.12, bf16[896,2048]{1,0:T(8,128)(2,1)S(1)} %get-tuple-element.19.kept_ref), custom_call_target="tpu_custom_call" | custom-call | tf_op jit(solution)/shard_map/pallas_call | solution.py:830
  211.7 4.9 %shard_map.63 = f32[1024,2048]{1,0:T(8,128)} custom-call(bf16[4,512,256]{2,1,0:T(8,128)(2,1)S(1)} %get-tuple-element.20.left_ref, bf16[2,8,256,256]{3,2,1,0:T(8,128)(2,1)S(1)} %get-tuple-element.21.right_ref), custom_call_target="tpu_custom_call" | custom-call | tf_op jit(solution)/shard_map/pallas_call | solution.py:798
Async XLA Ops:
  2.6 6.9 %copy-start.3 = (bf16[64,2048]{1,0:T(8,128)(2,1)S(1)}, bf16[64,2048]{1,0:T(8,128)(2,1)}, u32[]{:S(2)}) copy-start(bf16[64,2048]{1,0:T(8,128)(2,1)} %calib_ref.1) | copy-start | bytes 786436
  2.6 6.9 %copy-start.4 = (s32[5,7]{1,0:T(8,128)S(1)}, s32[5,7]{1,0:T(8,128)}, u32[]{:S(2)}) copy-start(s32[5,7]{1,0:T(8,128)} %stack.31.places_ref) | copy-start | bytes 424
  9.5 63.8 %copy-start.5 = (s32[7]{0:T(128)S(1)}, s32[7]{0:T(128)}, u32[]{:S(2)}) copy-start(s32[7]{0:T(128)} %blocks_ref.3) | copy-start | bytes 88
  9.5 2.2 %copy-start = (bf16[1024,2048]{1,0:T(8,128)(2,1)S(1)}, bf16[1024,2048]{1,0:T(8,128)(2,1)}, u32[]{:S(2)}) copy-start(bf16[1024,2048]{1,0:T(8,128)(2,1)} %weight_ref.3) | copy-start | bytes 12582916
  11.7 1.5 copy-start.2
  13.2 60.1 %copy-start.6 = (f32[1024,896]{1,0:T(8,128)S(1)}, f32[1024,896]{1,0:T(8,128)}, u32[]{:S(2)}) copy-start(f32[1024,896]{1,0:T(8,128)} %get-tuple-element.14) | copy-start | bytes 11010052
  73.3 131.8 %copy-start.1 = (bf16[1024,2048]{1,0:T(8,128)(2,1)S(1)}, bf16[1024,2048]{1,0:T(8,128)(2,1)}, u32[]{:S(2)}) copy-start(bf16[1024,2048]{1,0:T(8,128)(2,1)} %weight_ref.3) | copy-start | bytes 12582916

commit v6 on v5

--- a/solution.py
+++ b/solution.py
@@ -361,6 +361,7 @@
     place = ring_place(lax.axis_index("rows"))
     size = calib_ref.shape[0]
     all_calib_ref[span(place * size, size, 16), :] = calib_ref[...]
+    steps[1]()
     weight_copy.wait()
     for i in range(places_ref.shape[1]):
         at = lax.broadcasted_iota(jnp.int32, (BLOCK, weight_vmem.shape[0]), 1)
@@ -378,7 +379,6 @@
     used = count * BLOCK
     if kept_ref.shape[0] > used:
         kept_ref[used:, :] = jnp.zeros((kept_ref.shape[0] - used, kept_ref.shape[1]), kept_ref.dtype)
-    steps[1]()
     for at in range(max(len(steps) - 2, len(rings) - 1)):
         if at + 2 < len(steps):
             steps[at + 2]()

time: 217 us -> 216 us (level)
  no operation moved by 1% of the time
where the time goes in v6:
time: 216 us
  Pallas kernels  210 us (97%)
  local copies, waits for them, and re-layouts  4.3 us (2%)
    pallas_call x1, Pallas kernels, solve(): pl.pallas_call(solve_kernel, out_shape=outs, in_specs=[SMEM] + [VMEM] * 5...  132 us
    pallas_call x1, Pallas kernels, gather(): pl.pallas_call(functools.partial(gather_kernel, scale), out_shape=outs, i...  59.7 us
    pallas_call x1, Pallas kernels, pick_columns(): pl.pallas_call(pick_columns_kernel, out_shape=(jax.ShapeDtypeStruct((rows...  6.91 us
    pallas_call x1, Pallas kernels, prune(): pl.pallas_call(prune_kernel, out_shape=jax.ShapeDtypeStruct((rows, width)...  6.62 us
    pallas_call x1, Pallas kernels, gram_of(): pl.pallas_call(functools.partial(gram_kernel, row_parts, mp_parts), grid=...  4.85 us

profile of v6, /device:TPU:0, one launch (start us, length us, event | category | flops | bytes accessed | tf_op | source)
XLA Modules:
  0.0 216.3 jit_solution(1263234233633300919)
XLA Ops:
  0.6 0.7 fusion.1
  1.3 0.7 fusion.4
  2.0 0.6 stack.31.places_ref
  2.6 0.0 copy-start.3
  2.6 0.0 copy-start.4
  2.6 6.9 %shard_map.59 = (f32[1024,896]{1,0:T(8,128)}, f32[3584,128]{1,0:T(8,128)}) custom-call(s32[5,7]{1,0:T(8,128)} %stack.31.places_ref, f32[1024,2048]{1,0:T(8,128)} %factor_ref.1), custom_call_target="tpu_custom_call" | custom-call | tf_op jit(solution)/shard_map/pallas_call | solution.py:520
  9.5 0.0 copy-start.5
  9.5 0.0 copy-done.3
  9.5 0.0 copy-done.4
  9.5 0.0 copy-start
  9.5 2.2 %copy-done = bf16[1024,2048]{1,0:T(8,128)(2,1)S(1)} copy-done((bf16[1024,2048]{1,0:T(8,128)(2,1)S(1)}, bf16[1024,2048]{1,0:T(8,128)(2,1)}, u32[]{:S(2)}) %copy-start) | copy-done | bytes 4194328
  11.7 0.0 copy-start.2
  11.7 1.5 copy-done.2
  13.2 0.0 copy-start.6
  13.2 59.7 %shard_map.60 = (f32[3584,128]{1,0:T(8,128)S(1)}, bf16[896,2048]{1,0:T(8,128)(2,1)S(1)}, bf16[4,512,256]{2,1,0:T(8,128)(2,1)S(1)}, bf16[3584,128]{1,0:T(8,128)(2,1)S(1)}) custom-call(s32[5,7]{1,0:T(8,128)S(1)} %copy-done.4, f32[3584,128]{1,0:T(8,128)S(1)} %copy-done.2, bf16[64,2048]{1,0:T(8,128)(2,1)S(1)} %copy-done.3, bf16[1024,2048]{1,0:T(8,128)(2,1)S(1)} %copy-done), custom_call_target="tpu_custom_call" | custom-call | tf_op jit(solution)/shard_map/pallas_call | solution.py:446
  72.9 0.0 copy-done.5
  72.9 0.0 copy-done.6
  72.9 0.0 copy-start.1
  72.9 131.9 %shard_map.61 = (bf16[4,512,256]{2,1,0:T(8,128)(2,1)S(1)}, bf16[2,8,256,256]{3,2,1,0:T(8,128)(2,1)S(1)}, bf16[4,256,896]{2,1,0:T(8,128)(2,1)S(1)}, bf16[896,2048]{1,0:T(8,128)(2,1)S(1)}) custom-call(s32[7]{0:T(128)S(1)} %copy-done.5, f32[3584,128]{1,0:T(8,128)S(1)} %get-tuple-element.13.low_ref, f32[4,256,896]{2,1,0:T(8,128)S(1)} %bitcast.13, ...), custom_call_target="tpu_custom_call" | custom-call | flops 60000002048 | bytes 6422528 | tf_op jit(solution)/shard_map/pallas_call | solution.py:757
  204.8 0.0 copy-done.1
  204.8 6.6 %shard_map.62 = bf16[1024,2048]{1,0:T(8,128)(2,1)} custom-call(s32[7]{0:T(128)S(1)} %copy-done.5, bf16[1024,2048]{1,0:T(8,128)(2,1)S(1)} %copy-done.1, bf16[1024,896]{1,0:T(8,128)(2,1)S(1)} %bitcast.12, bf16[896,2048]{1,0:T(8,128)(2,1)S(1)} %get-tuple-element.19.kept_ref), custom_call_target="tpu_custom_call" | custom-call | tf_op jit(solution)/shard_map/pallas_call | solution.py:830
  211.4 4.9 %shard_map.63 = f32[1024,2048]{1,0:T(8,128)} custom-call(bf16[4,512,256]{2,1,0:T(8,128)(2,1)S(1)} %get-tuple-element.20.left_ref, bf16[2,8,256,256]{3,2,1,0:T(8,128)(2,1)S(1)} %get-tuple-element.21.right_ref), custom_call_target="tpu_custom_call" | custom-call | tf_op jit(solution)/shard_map/pallas_call | solution.py:798
Async XLA Ops:
  2.6 6.9 %copy-start.3 = (bf16[64,2048]{1,0:T(8,128)(2,1)S(1)}, bf16[64,2048]{1,0:T(8,128)(2,1)}, u32[]{:S(2)}) copy-start(bf16[64,2048]{1,0:T(8,128)(2,1)} %calib_ref.1) | copy-start | bytes 786436
  2.6 6.9 %copy-start.4 = (s32[5,7]{1,0:T(8,128)S(1)}, s32[5,7]{1,0:T(8,128)}, u32[]{:S(2)}) copy-start(s32[5,7]{1,0:T(8,128)} %stack.31.places_ref) | copy-start | bytes 424
  9.5 63.4 %copy-start.5 = (s32[7]{0:T(128)S(1)}, s32[7]{0:T(128)}, u32[]{:S(2)}) copy-start(s32[7]{0:T(128)} %blocks_ref.3) | copy-start | bytes 88
  9.5 2.2 %copy-start = (bf16[1024,2048]{1,0:T(8,128)(2,1)S(1)}, bf16[1024,2048]{1,0:T(8,128)(2,1)}, u32[]{:S(2)}) copy-start(bf16[1024,2048]{1,0:T(8,128)(2,1)} %weight_ref.3) | copy-start | bytes 12582916
  11.7 1.5 copy-start.2
  13.2 59.7 %copy-start.6 = (f32[1024,896]{1,0:T(8,128)S(1)}, f32[1024,896]{1,0:T(8,128)}, u32[]{:S(2)}) copy-start(f32[1024,896]{1,0:T(8,128)} %get-tuple-element.14) | copy-start | bytes 11010052
  72.9 131.9 %copy-start.1 = (bf16[1024,2048]{1,0:T(8,128)(2,1)S(1)}, bf16[1024,2048]{1,0:T(8,128)(2,1)}, u32[]{:S(2)}) copy-start(bf16[1024,2048]{1,0:T(8,128)(2,1)} %weight_ref.3) | copy-start | bytes 12582916
